TPU v7x, 256 devices: a whole 4x4x8 slice. The times are simulated.
256 devices in a mesh: redist: 128 (over y, z, x), rep: 2 (over core).
Axes of the slice: x: 4, y: 4, z: 8, core: 2. Of those that a mesh axis runs over, the one named last changes fastest.
Arguments:
- amplitudes: float32 [8, 256, 2, 3840], P(None, 'redist', 'rep'), may hold values from -6 to 6
- integrals: float32 [128, 1920, 2, 960], P('redist', None, 'rep'), may hold values from -0.0625 to 0.0625
- pair_count: int32 [8], replicated, may hold values from 5760 to 7680, as said below
Outputs:
- cycle_term: float32 [8, 256, 2, 3840], P(None, 'redist', 'rep')
Inputs may be any that keep to these rules, and one draw needn't show every extreme that they name: `pair_count`: each block has at least 5760 live pair slots; some block has all 7680 live.
All inputs are finite; a program needn't handle non-finite values.
Results may differ from a plain program's by a relative error of at most 0.00007.
Values sent between devices are 32-bit elements; how exact they have to be, the bound alone decides.
No kernel may reach another device: no remote copies, remote signals or barrier semaphores. Data moves between devices by JAX's collectives and lax.ppermute only.
A program may use at most 64 MiB of HBM per device.

v0:
```python
import jax
import jax.numpy as jnp
from jax import lax
from jax.sharding import PartitionSpec as P

NBLK = 8


def arrange(moved, rows, jb_split, kc_split, col_width, half_slots):
    summed = moved.reshape(NBLK, jb_split, kc_split, rows, col_width).sum(axis=2)
    return summed.transpose(0, 2, 1, 3).reshape(NBLK, rows, 2, half_slots)


def on_device(amplitudes, integrals, pair_count):
    half_slots = amplitudes.shape[3]
    row_count = amplitudes.shape[1]
    col_width = integrals.shape[1]
    kc_width = integrals.shape[3]
    kc_split = half_slots // kc_width
    jb_split = 2 * half_slots // col_width
    device_count = lax.axis_size("redist")
    half_index = lax.axis_index("rep")
    slot_index = half_index * half_slots + lax.iota(jnp.int32, half_slots)
    live_mask = (slot_index[None, :] < pair_count[:, None]).astype(jnp.float32)
    masked = amplitudes[:, :, 0, :] * live_mask[:, None, :]
    pieces = masked.reshape(NBLK, row_count, kc_split, kc_width).transpose(0, 2, 1, 3)
    outgoing = jnp.broadcast_to(
        pieces[:, None], (NBLK, jb_split, kc_split, row_count, kc_width)
    ).reshape(device_count, row_count, kc_width)
    tile_matrix = integrals[0, :, 0, :]
    partial_value = jnp.einsum(
        "srk,jk->srj",
        lax.all_to_all(outgoing, "redist", split_axis=0, concat_axis=0, tiled=True),
        tile_matrix,
        precision=lax.Precision.HIGHEST,
        preferred_element_type=jnp.float32,
    )
    moved = lax.all_to_all(partial_value, "redist", split_axis=0, concat_axis=0, tiled=True)
    arranged = arrange(moved, row_count, jb_split, kc_split, col_width, half_slots)
    result = lax.psum_scatter(arranged, "rep", scatter_dimension=2, tiled=True)
    return result * live_mask[:, None, None, :]


def solution(mesh):
    placed = (P(None, "redist", "rep", None), P("redist", None, "rep", None), P())
    return jax.shard_map(
        on_device,
        mesh=mesh,
        in_specs=placed,
        out_specs=P(None, "redist", "rep", None),
        check_vma=False,
    )
```

profile of v0, /device:TPU:1, one launch (start us, length us, event | category | flops | bytes accessed | tf_op | source)
XLA Modules:
  0.0 143.1 jit_solution(7868361592408624490)
XLA Ops:
  6.5 0.0 reduce-scatter.2.cloned.1.call-start
  6.5 1.7 %reduce = f32[8,2,3840]{2,1,0:T(2,128)S(1)} reduce(f32[8,2,1,3840]{3,2,1,0:T(1,128)} %param.3, f32[]{:T(128)} %constant.12), dimensions={2}, to_apply=%param.3.reduce_sub_computation | reduce | bytes 491524 | tf_op args[0]
  8.2 0.3 squeeze.6
  8.5 0.7 compare_convert_fusion
  9.3 0.1 multiply_bitcast_fusion
  9.4 0.2 copy.7
  9.6 0.5 broadcast_in_dim.2
  10.1 43.4 %all_to_all.10 = f32[128,2,960]{2,1,0:T(2,128)S(1)} all-to-all(f32[128,2,960]{2,1,0:T(2,128)S(1)} %bitcast.15), channel_id=1, replica_groups=mesh['redist'=128,'rep'=2] {'redist'}, dimensions={0} | all-to-all | bytes 1966080 | tf_op jit(solution)/shard_map/all_to_all | solution.py:33
  53.4 9.9 %fusion = f32[128,2,1920]{2,0,1:T(8,128)S(1)} fusion(f32[1,1920,1,960]{1,3,2,0:T(8,128)} %param.4, f32[128,2,960]{2,1,0:T(2,128)S(1)} %all_to_all.10), kind=kOutput, calls=%fused_computation | convolution fusion | flops 5662310400 | bytes 10321920 | tf_op jit(solution)/shard_map/srk,jk->srj/dot_general | solution.py:31
  63.3 1.5 %copy.9 = f32[128,2,1920]{2,1,0:T(2,128)S(1)} copy(f32[128,2,1920]{2,0,1:T(8,128)S(1)} %fusion) | data formatting | bytes 3932160 | tf_op jit(solution)/shard_map/srk,jk->srj/dot_general | solution.py:31
  64.8 55.4 %all_to_all.11 = f32[128,2,1920]{2,1,0:T(2,128)S(1)} all-to-all(f32[128,2,1920]{2,1,0:T(2,128)S(1)} %copy.9), channel_id=1, replica_groups=mesh['redist'=128,'rep'=2] {'redist'}, dimensions={0} | all-to-all | bytes 3932160 | tf_op jit(solution)/shard_map/all_to_all | solution.py:38
  120.2 0.7 bitcast_reduce_fusion
  120.9 0.0 copy-start
  120.9 0.1 copy.17
  121.0 0.4 reshape.69
  121.5 0.8 copy.11
  122.3 0.0 reduce-scatter.2.cloned.1.call-update
  122.3 0.0 copy-done
  122.3 0.1 compare_convert_fusion.1
  122.4 11.9 %reduce-scatter.2.cloned.1.call-done = f32[8,2,1,3840]{3,0,1,2:T(8,128)} async-done(((f32[8,2,2,3840]{3,0,1,2:T(8,128)}), f32[8,2,1,3840]{3,0,1,2:T(8,128)}) %reduce-scatter.2.cloned.1.call-update) | async-done | bytes 245776 | tf_op jit(solution)/shard_map/reduce_scatter | solution.py:40
  134.3 1.0 broadcast_multiply_fusion
  135.3 0.9 copy.12
  (2 shorter events, 0.0 us)
Async XLA Ops:
  6.5 127.8 %reduce-scatter.2.cloned.1.call-start = ((), (), s32[]{:S(2)}) async-start(), calls=%async_computation.3 | async-start | bytes 737280 | tf_op jit(solution)/shard_map/reduce_scatter | solution.py:40
  120.9 1.4 copy-start
Sparse Core Ops, SparseCore 0:
  122.4 11.8 reduce-scatter.1
where the time goes:
time: 143 us
  blocking collectives  98.8 us (69%)
  between operations  13.5 us (9%)
  waiting for transfers between devices  11.9 us (8%)
  matrix products  9.86 us (7%)
  local copies, waits for them, and re-layouts  4.83 us (3%)
  other arithmetic  4.2 us (3%)
    all_to_all x1, blocking collectives, on_device(): lax.all_to_all(partial_value, 'redist', split_axis=0, concat_axis=0, tile...  55.4 us
    all_to_all x1, blocking collectives, on_device(): lax.all_to_all(outgoing, 'redist', split_axis=0, concat_axis=0, tiled=True)  43.4 us
    reduce_scatter x1, waiting for transfers between devices, on_device(): result = lax.psum_scatter(arranged, 'rep', scatter_dimension=2, tiled=True)  11.9 us
    dot_general x1, matrix products, on_device(): jnp.einsum('srk,jk->srj', lax.all_to_all(outgoing, 'redist', split_axis=0...  9.86 us
  transfers between devices with their start and end apart: 1, of which 1 were waited for; matrix products, arithmetic and copies ran while one was open for 0% of the time, Pallas kernels for 0%

commit v1 on v0

v1 whole, which is shorter than its diff:
```python
import jax
import jax.numpy as jnp
from jax import lax
from jax.sharding import Mesh, PartitionSpec as P

NBLK = 8
YZ = ("y", "zh", "zl")
YZX = ("y", "zh", "zl", "x")
SWAP = [(0, 1), (1, 0)]


def on_device(amplitudes, integrals, pair_count):
    half_slots = amplitudes.shape[3]
    rows = amplitudes.shape[1]
    col_width = integrals.shape[1]
    kc_width = integrals.shape[3]
    kc_split = half_slots // kc_width
    jb_split = 2 * half_slots // col_width
    owners = lax.axis_size("y") * lax.axis_size("zh") * lax.axis_size("zl")
    half = lax.axis_index("rep")
    first = half == 0
    slot_index = half * half_slots + lax.iota(jnp.int32, half_slots)
    live_mask = (slot_index[None, :] < pair_count[:, None]).astype(jnp.float32)
    masked = amplitudes[:, :, 0, :] * live_mask[:, None, :]
    pieces = masked.reshape(NBLK, rows, kc_split, kc_width).transpose(0, 2, 1, 3)
    outgoing = jnp.broadcast_to(
        pieces[:, None], (NBLK, jb_split, kc_split, rows, kc_width)
    ).reshape(-1, rows, kc_width)
    arrived = lax.all_to_all(outgoing, YZX, split_axis=0, concat_axis=0, tiled=True)
    tile = integrals[0, :, 0, :]
    partial = jnp.einsum(
        "srk,jk->srj",
        arrived,
        tile,
        precision=lax.Precision.HIGH,
        preferred_element_type=jnp.float32,
    )
    width = col_width // 2
    low, high = partial[:, :, :width], partial[:, :, width:]
    away = jnp.where(first, high, low)
    own = jnp.where(first, low, high)
    pair_sum = own + lax.ppermute(away, "rep", SWAP)
    by_x = pair_sum.reshape(owners, -1, rows, width).transpose(1, 0, 2, 3)
    gathered = lax.all_to_all(by_x, "x", split_axis=0, concat_axis=0, tiled=True)
    summed = gathered.sum(axis=0)
    moved = lax.all_to_all(summed, YZ, split_axis=0, concat_axis=0, tiled=True)
    by_half = moved.reshape(NBLK, 2, jb_split // 2, rows, width)
    mine = jnp.where(first, by_half[:, 0], by_half[:, 1])
    theirs = jnp.where(first, by_half[:, 1], by_half[:, 0])
    other = lax.ppermute(theirs, "rep", SWAP)
    low = jnp.where(first, mine, other)
    high = jnp.where(first, other, mine)
    both = jnp.stack([low, high], axis=2)
    result = both.transpose(0, 3, 1, 2, 4).reshape(NBLK, rows, half_slots)
    return (result * live_mask[:, None, :])[:, :, None, :]


def solution(mesh):
    fine = Mesh(
        mesh.devices.reshape(4, 2, 4, 4, 2), ("y", "zh", "zl", "x", "rep")
    )
    placed = (P(None, YZX, "rep", None), P(YZX, None, "rep", None), P())
    return jax.shard_map(
        on_device,
        mesh=fine,
        in_specs=placed,
        out_specs=P(None, YZX, "rep", None),
        check_vma=False,
    )
```

time: 143 us -> 103 us (0.72)
  blocking collectives: 98.8 us -> 16.9 us
  starting transfers between devices: 0.01 us -> 28.5 us
  waiting for transfers between devices: 11.9 us -> 40 us
  between operations: 13.5 us -> 0.14 us
    all_to_all x2 -> x1, blocking collectives: 98.8 us -> 16.9 us  [on_device(): lax.all_to_all(by_x, 'x', split_axis=0, concat_axis=0, tiled=True)]
    all_to_all x0 -> x2, waiting for transfers between devices: none -> 36.9 us  [the longest x1 27.2 us: on_device(): lax.all_to_all(outgoing, YZX, split_axis=0, concat_axis=0, tiled=True)]
    all_to_all x0 -> x2, starting transfers between devices: none -> 21.1 us  [the longest x1 16.3 us: on_device(): lax.all_to_all(outgoing, YZX, split_axis=0, concat_axis=0, tiled=True)]
    reduce_scatter x1 -> x0, waiting for transfers between devices: 11.9 us -> none  [on_device(): result = lax.psum_scatter(arranged, 'rep', scatter_dimension=2, tiled=True)]
    ppermute x0 -> x2, starting transfers between devices: none -> 7.4 us  [the longest x1 3.71 us: on_device(): pair_sum = own + lax.ppermute(away, 'rep', SWAP)]
    ppermute x0 -> x2, waiting for transfers between devices: none -> 3.1 us  [the longest x1 2.19 us: on_device(): pair_sum = own + lax.ppermute(away, 'rep', SWAP)]
    dot_general x1 -> x0, local copies, waits for them, and re-layouts: 1.52 us -> none  [on_device(): jnp.einsum('srk,jk->srj', lax.all_to_all(outgoing, 'redist', split_axis=0...]
  transfers between devices with their start and end apart: 1 -> 4, of which waited for: 1 -> 4; matrix products, arithmetic and copies ran while one was open for 0% -> 0% of each run, Pallas kernels for 0% -> 0%
where the time goes in v1:
time: 103 us
  waiting for transfers between devices  40 us (39%)
  starting transfers between devices  28.5 us (28%)
  blocking collectives  16.9 us (16%)
  matrix products  8.53 us (8%)
  other arithmetic  4.48 us (4%)
  local copies, waits for them, and re-layouts  4.25 us (4%)
    all_to_all x1, waiting for transfers between devices, on_device(): lax.all_to_all(outgoing, YZX, split_axis=0, concat_axis=0, tiled=True)  27.2 us
    all_to_all x1, blocking collectives, on_device(): lax.all_to_all(by_x, 'x', split_axis=0, concat_axis=0, tiled=True)  16.9 us
    all_to_all x1, starting transfers between devices, on_device(): lax.all_to_all(outgoing, YZX, split_axis=0, concat_axis=0, tiled=True)  16.3 us
    all_to_all x1, waiting for transfers between devices, on_device(): moved = lax.all_to_all(summed, YZ, split_axis=0, concat_axis=0, tiled=True)  9.64 us
    dot_general x1, matrix products, on_device(): jnp.einsum('srk,jk->srj', arrived, tile, precision=lax.Precision.HIGH, pr...  8.53 us
    all_to_all x1, starting transfers between devices, on_device(): moved = lax.all_to_all(summed, YZ, split_axis=0, concat_axis=0, tiled=True)  4.77 us
    ppermute x1, starting transfers between devices, on_device(): pair_sum = own + lax.ppermute(away, 'rep', SWAP)  3.71 us
    ppermute x1, starting transfers between devices, on_device(): other = lax.ppermute(theirs, 'rep', SWAP)  3.69 us
  transfers between devices with their start and end apart: 4, of which 4 were waited for; matrix products, arithmetic and copies ran while one was open for 0% of the time, Pallas kernels for 0%

profile of v1, /device:TPU:1, one launch (start us, length us, event | category | flops | bytes accessed | tf_op | source)
XLA Modules:
  0.0 102.8 jit_solution(10969920210144423862)
XLA Ops:
  0.0 1.7 %reduce = f32[8,2,3840]{2,1,0:T(2,128)S(1)} reduce(f32[8,2,1,3840]{3,2,1,0:T(1,128)} %param.3, f32[]{:T(128)} %constant.14), dimensions={2}, to_apply=%param.3.reduce_sub_computation | reduce | bytes 491524 | tf_op args[0]
  1.7 0.3 squeeze.4
  2.0 0.7 compare_convert_fusion
  2.8 0.1 multiply_bitcast_fusion
  2.8 0.2 copy.34
  3.0 1.4 %broadcast_in_dim.2 = f32[8,4,4,2,960]{4,3,2,1,0:T(2,128)} broadcast(f32[8,4,2,960]{3,2,1,0:T(2,128)S(1)} %copy.34), dimensions={0,2,3,4} | broadcast | bytes 1228800 | tf_op jit(solution)/shard_map/broadcast_in_dim | solution.py:26
  4.5 16.3 %all-to-all-start = ((f32[128,2,960]{2,1,0:T(2,128)}), f32[128,2,960]{2,1,0:T(2,128)S(1)}, u32[]{:S(2)}, u32[]{:S(2)}) async-start(f32[128,2,960]{2,1,0:T(2,128)} %bitcast.1), calls=%async_computation | async-start | bytes 2097152 | tf_op jit(solution)/shard_map/all_to_all | solution.py:29
  20.8 27.2 %all-to-all-done = f32[128,2,960]{2,1,0:T(2,128)S(1)} async-done(((f32[128,2,960]{2,1,0:T(2,128)}), f32[128,2,960]{2,1,0:T(2,128)S(1)}, u32[]{:S(2)}, u32[]{:S(2)}) %all-to-all-start) | async-done | bytes 983072 | tf_op jit(solution)/shard_map/all_to_all | solution.py:29
  48.1 8.5 %fusion = f32[128,2,1920]{0,2,1:T(8,128)S(1)} fusion(f32[1,1920,1,960]{1,3,2,0:T(8,128)} %param.4, f32[128,2,960]{2,1,0:T(2,128)S(1)} %all-to-all-done), kind=kOutput, calls=%fused_computation | convolution fusion | flops 2831155200 | bytes 10321920 | tf_op jit(solution)/shard_map/srk,jk->srj/dot_general | solution.py:31
  56.6 0.0 copy-start
  56.6 0.1 slice_select_fusion
  56.7 3.7 %collective-permute-start = (f32[128,2,960]{0,2,1:T(8,128)S(1)}, f32[128,2,960]{0,2,1:T(8,128)S(1)}, u32[]{:S(2)}, u32[]{:S(2)}) collective-permute-start(f32[128,2,960]{0,2,1:T(8,128)S(1)} %slice_select_fusion), channel_id=1, source_target_pairs={{0,1},{1,0},{2,3},{3,2},{4,5},{5,4},{6,7},{7,6},{8,9},{9,8},{10,11... | collective-permute-start | bytes 2949128 | tf_op jit(solution)/shard_map/ppermute | solution.py:42
  60.4 2.2 %collective-permute-done = f32[128,2,960]{0,2,1:T(8,128)S(1)} collective-permute-done((f32[128,2,960]{0,2,1:T(8,128)S(1)}, f32[128,2,960]{0,2,1:T(8,128)S(1)}, u32[]{:S(2)}, u32[]{:S(2)}) %collective-permute-start) | collective-permute-done | bytes 983072 | tf_op jit(solution)/shard_map/ppermute | solution.py:42
  62.6 0.2 select_add_fusion
  62.8 0.7 copy.38
  63.6 0.1 copy.39
  63.6 16.9 %all_to_all.15 = f32[4,32,2,960]{3,2,1,0:T(2,128)S(1)} all-to-all(f32[4,32,2,960]{3,2,1,0:T(2,128)S(1)} %copy.39), channel_id=1, replica_groups=mesh['y'=4,'zh'=2,'zl'=4,'x'=4,'rep'=2] {'x'}, dimensions={0} | all-to-all | bytes 1966080 | tf_op jit(solution)/shard_map/all_to_all | solution.py:44
  80.5 1.3 %reduce_sum.9 = f32[32,2,960]{2,1,0:T(2,128)} reduce(f32[4,32,2,960]{3,2,1,0:T(2,128)S(1)} %all_to_all.15, f32[]{:T(128)} %constant.11.clone.1), dimensions={0}, to_apply=%region_0.1 | reduce | flops 184320 | bytes 1228804 | tf_op jit(solution)/shard_map/reduce_sum | solution.py:45
  81.8 4.8 %all-to-all-start.2 = ((f32[32,2,960]{2,1,0:T(2,128)}), f32[32,2,960]{2,1,0:T(2,128)S(1)}, u32[]{:S(2)}, u32[]{:S(2)}) async-start(f32[32,2,960]{2,1,0:T(2,128)} %reduce_sum.9), calls=%async_computation.2 | async-start | bytes 524288 | tf_op jit(solution)/shard_map/all_to_all | solution.py:46
  86.6 9.6 %all-to-all-done.2 = f32[32,2,960]{2,1,0:T(2,128)S(1)} async-done(((f32[32,2,960]{2,1,0:T(2,128)}), f32[32,2,960]{2,1,0:T(2,128)S(1)}, u32[]{:S(2)}, u32[]{:S(2)}) %all-to-all-start.2) | async-done | bytes 245792 | tf_op jit(solution)/shard_map/all_to_all | solution.py:46
  96.3 0.1 fusion.3
  96.3 3.7 %collective-permute-start.1 = (f32[8,2,2,960]{3,2,1,0:T(2,128)S(1)}, f32[8,2,2,960]{3,2,1,0:T(2,128)S(1)}, u32[]{:S(2)}, u32[]{:S(2)}) collective-permute-start(f32[8,2,2,960]{3,2,1,0:T(2,128)S(1)} %fusion.3), channel_id=1, source_target_pairs={{0,1},{1,0},{2,3},{3,2},{4,5},{5,4},{6,7},{7,6},{8,9},{9,8},{10,11... | collective-permute-start | bytes 368648 | tf_op jit(solution)/shard_map/ppermute | solution.py:50
  100.0 0.0 copy-done
  100.0 0.1 compare_convert_fusion.1
  100.1 0.9 collective-permute-done.1
  101.0 0.1 select_bitcast_fusion.1
  101.1 0.1 maximum_bitcast_fusion
  101.3 0.2 copy.44
  101.5 0.3 reshape.69
  101.8 0.9 copy.45
  (3 shorter events, 0.0 us)
Async XLA Ops:
  4.5 43.6 %all-to-all-start = ((f32[128,2,960]{2,1,0:T(2,128)}), f32[128,2,960]{2,1,0:T(2,128)S(1)}, u32[]{:S(2)}, u32[]{:S(2)}) async-start(f32[128,2,960]{2,1,0:T(2,128)} %bitcast.1), calls=%async_computation | async-start | bytes 2097152 | tf_op jit(solution)/shard_map/all_to_all | solution.py:29
  56.6 43.4 %copy-start = (s32[8]{0:T(128)S(1)}, s32[8]{0:T(128)}, u32[]{:S(2)}) copy-start(s32[8]{0:T(128)} %param.5) | copy-start | bytes 100
  56.7 5.9 %collective-permute-start = (f32[128,2,960]{0,2,1:T(8,128)S(1)}, f32[128,2,960]{0,2,1:T(8,128)S(1)}, u32[]{:S(2)}, u32[]{:S(2)}) collective-permute-start(f32[128,2,960]{0,2,1:T(8,128)S(1)} %slice_select_fusion), channel_id=1, source_target_pairs={{0,1},{1,0},{2,3},{3,2},{4,5},{5,4},{6,7},{7,6},{8,9},{9,8},{10,11... | collective-permute-start | bytes 2949128 | tf_op jit(solution)/shard_map/ppermute | solution.py:42
  81.8 14.4 %all-to-all-start.2 = ((f32[32,2,960]{2,1,0:T(2,128)}), f32[32,2,960]{2,1,0:T(2,128)S(1)}, u32[]{:S(2)}, u32[]{:S(2)}) async-start(f32[32,2,960]{2,1,0:T(2,128)} %reduce_sum.9), calls=%async_computation.2 | async-start | bytes 524288 | tf_op jit(solution)/shard_map/all_to_all | solution.py:46
  96.3 4.7 %collective-permute-start.1 = (f32[8,2,2,960]{3,2,1,0:T(2,128)S(1)}, f32[8,2,2,960]{3,2,1,0:T(2,128)S(1)}, u32[]{:S(2)}, u32[]{:S(2)}) collective-permute-start(f32[8,2,2,960]{3,2,1,0:T(2,128)S(1)} %fusion.3), channel_id=1, source_target_pairs={{0,1},{1,0},{2,3},{3,2},{4,5},{5,4},{6,7},{7,6},{8,9},{9,8},{10,11... | collective-permute-start | bytes 368648 | tf_op jit(solution)/shard_map/ppermute | solution.py:50

commit v2 on v0

v2 whole, which is shorter than its diff:
```python
import functools

import jax
import jax.numpy as jnp
from jax import lax
from jax.experimental import pallas as pl
from jax.experimental.pallas import tpu as pltpu
from jax.sharding import Mesh, PartitionSpec as P

NBLK = 8
YZX = ("y", "z", "x")
SWAP = [(0, 1), (1, 0)]
RING = 4
DEEP = 8
OWNERS = 32
LANES = 128
PART = 1024
STEP = 896
CHUNKS = 1
VMEM = pl.BlockSpec(memory_space=pltpu.VMEM)
SMEM = pl.BlockSpec(memory_space=pltpu.SMEM)
ANY = pl.BlockSpec(memory_space=pl.ANY)


def shift(value, axis, by):
    n = lax.axis_size(axis)
    return lax.ppermute(value, axis, [(i, (i + by) % n) for i in range(n)])


def pick(value, index, axis=0):
    return lax.dynamic_index_in_dim(value, index, axis, keepdims=False)


def params(mib):
    return pltpu.CompilerParams(vmem_limit_bytes=mib << 20)


def cost(flops, nbytes):
    return pl.CostEstimate(flops=flops, bytes_accessed=nbytes, transcendentals=0)


def live_limit(count_ref):
    return count_ref[lax.axis_index("y") * 2 + lax.axis_index("z") // RING]


def prepare_kernel(amp_ref, out_hbm, piece_ref, sems):
    width = piece_ref.shape[3]
    for g in range(NBLK):
        for r in range(2):
            row = amp_ref[g, r]
            for k in range(RING):
                piece_ref[g, k, r : r + 1, :] = row[:, k * width : (k + 1) * width]
    copies = [
        pltpu.make_async_copy(piece_ref, out_hbm.at[:, j], sems.at[j]) for j in range(RING)
    ]
    for copy in copies:
        copy.start()
    for copy in copies:
        copy.wait()


def prepare(amplitudes, width):
    return pl.pallas_call(
        prepare_kernel,
        in_specs=[VMEM],
        out_specs=ANY,
        out_shape=jax.ShapeDtypeStruct((NBLK, RING, RING, 2, width), jnp.float32),
        scratch_shapes=[
            pltpu.VMEM((NBLK, RING, 2, width), jnp.float32),
            pltpu.SemaphoreType.DMA((RING,)),
        ],
        cost_estimate=cost(0, 5 * 4 * amplitudes.size),
        compiler_params=params(56),
        name="prepare",
    )(amplitudes)


def arrange_kernel(count_ref, got_ref, out_ref):
    width = got_ref.shape[3]
    base = lax.axis_index("rep") * (RING * width) + lax.axis_index("x") * width
    slot = lax.broadcasted_iota(jnp.int32, (1, width), 1) + base
    live = (slot < live_limit(count_ref)).astype(jnp.float32)
    for x in range(RING):
        for r in range(2):
            at = (x * 2 + r) * OWNERS
            out_ref[at : at + OWNERS, :] = got_ref[:, x, r, :] * live


def arrange(pair_count, got):
    width = got.shape[3]
    rows = OWNERS * RING * 2
    return pl.pallas_call(
        arrange_kernel,
        in_specs=[SMEM, VMEM],
        out_specs=VMEM,
        out_shape=jax.ShapeDtypeStruct((rows, width), jnp.float32),
        cost_estimate=cost(0, 8 * rows * width),
        compiler_params=params(16),
        name="arrange",
    )(pair_count, got)


def gather_kernel(*refs):
    out_ref = refs[-1]
    width = PART // CHUNKS
    for c in range(CHUNKS):
        p = refs[c * RING : (c + 1) * RING]
        for r in range(2):
            at = slice(r * OWNERS, (r + 1) * OWNERS)
            total = (p[0][at] + p[1][at]) + (p[2][at] + p[3][at])
            out_ref[:, r, c * width : (c + 1) * width] = total


def gather(parts):
    return pl.pallas_call(
        gather_kernel,
        in_specs=[VMEM] * len(parts),
        out_specs=VMEM,
        out_shape=jax.ShapeDtypeStruct((OWNERS, 2, PART), jnp.float32),
        compiler_params=params(16),
        cost_estimate=cost(0, 5 * 4 * OWNERS * 2 * PART),
        name="gather_rows",
    )(*parts)


def final_kernel(moved_ref, other_ref, out_ref):
    def write(low_of, high_of):
        for g in range(NBLK):
            for r in range(2):
                for j in range(2):
                    base = j * (PART + STEP)
                    out_ref[g, r, :, base : base + PART] = low_of(g, j, r)
                    out_ref[g, r, :, base + PART : base + PART + STEP] = high_of(g, j, r)[:, LANES:]

    half = lax.axis_index("rep")

    @pl.when(half == 0)
    def _():
        write(
            lambda g, j, r: moved_ref[g, j, r : r + 1, :],
            lambda g, j, r: other_ref[g, j, r : r + 1, :],
        )

    @pl.when(half == 1)
    def _():
        write(
            lambda g, j, r: other_ref[g, j, r : r + 1, :],
            lambda g, j, r: moved_ref[g, 2 + j, r : r + 1, :],
        )


def final(moved, other, shape):
    return pl.pallas_call(
        final_kernel,
        in_specs=[VMEM, VMEM],
        out_specs=VMEM,
        out_shape=jax.ShapeDtypeStruct(shape, jnp.float32),
        compiler_params=params(16),
        name="final_rows",
    )(moved, other)


def contract(rows, integrals, pair_count):
    width = integrals.shape[1]
    limit = pick(pair_count, lax.axis_index("y") * 2 + lax.axis_index("z") // RING)
    column = (lax.axis_index("z") % RING) * width + lax.iota(jnp.int32, width)
    keep = (column < limit).astype(jnp.float32)
    partial = jnp.einsum(
        "rk,jk->rj",
        rows,
        integrals[0, :, 0, :],
        precision=lax.Precision.HIGH,
        preferred_element_type=jnp.float32,
    )
    partial = partial * keep[None, :]
    return partial[:, :PART], partial[:, STEP:]


def on_device(amplitudes, integrals, pair_count):
    kc_width = integrals.shape[3]
    half = lax.axis_index("rep")
    my_x = lax.axis_index("x")
    outgoing = prepare(amplitudes, kc_width).reshape(-1, 2, kc_width)
    got = lax.all_to_all(outgoing, YZX, split_axis=0, concat_axis=0, tiled=True)
    rows = arrange(pair_count, got.reshape(OWNERS, RING, 2, kc_width))
    low, high = contract(rows, integrals, pair_count)
    first = half == 0
    pair_sum = jnp.where(first, low, high) + lax.ppermute(jnp.where(first, high, low), "rep", SWAP)
    pair_sum = pair_sum.reshape(RING, 2 * OWNERS, PART)
    parts = [pick(pair_sum, my_x)]
    for s in range(1, RING):
        parts.append(shift(pick(pair_sum, (my_x + s) % RING), "x", s))
    leaving = gather(parts)
    moved = lax.all_to_all(leaving, ("y", "z"), split_axis=0, concat_axis=0, tiled=True)
    moved = moved.reshape(NBLK, RING, 2, PART)
    theirs = lax.dynamic_slice_in_dim(moved, (1 - half) * 2, 2, axis=1)
    other = lax.ppermute(theirs, "rep", SWAP)
    return final(moved, other, amplitudes.shape)


def solution(mesh):
    fine = Mesh(mesh.devices.reshape(4, 8, 4, 2), ("y", "z", "x", "rep"))
    placed = (P(None, YZX, "rep", None), P(YZX, None, "rep", None), P())
    return jax.shard_map(
        on_device,
        mesh=fine,
        in_specs=placed,
        out_specs=P(None, YZX, "rep", None),
        check_vma=False,
    )
```

time: 143 us -> 95.6 us (0.67)
  blocking collectives: 98.8 us -> 0 us
  waiting for transfers between devices: 11.9 us -> 50.1 us
  starting transfers between devices: 0.01 us -> 31.8 us
  between operations: 13.5 us -> 0.12 us
  Pallas kernels: 0 us -> 4.41 us
  local copies, waits for them, and re-layouts: 4.83 us -> 0.68 us
  matrix products: 9.86 us -> 6.25 us
  other arithmetic: 4.2 us -> 1.94 us
    all_to_all x2 -> x0, blocking collectives: 98.8 us -> none  [the longest x1 55.4 us: on_device(): lax.all_to_all(partial_value, 'redist', split_axis=0, concat_axis=0, tile...]
    all_to_all x0 -> x2, waiting for transfers between devices: none -> 35.6 us  [the longest x1 26 us: on_device(): got = lax.all_to_all(outgoing, YZX, split_axis=0, concat_axis=0, tiled=True)]
    all_to_all x0 -> x2, starting transfers between devices: none -> 20.8 us  [the longest x1 16.3 us: on_device(): got = lax.all_to_all(outgoing, YZX, split_axis=0, concat_axis=0, tiled=True)]
    ppermute x0 -> x5, waiting for transfers between devices: none -> 14.5 us  [the longest x3 11 us: shift(): return lax.ppermute(value, axis, [(i, (i + by) % n) for i in range(n)])]
    reduce_scatter x1 -> x0, waiting for transfers between devices: 11.9 us -> none  [on_device(): result = lax.psum_scatter(arranged, 'rep', scatter_dimension=2, tiled=True)]
    ppermute x0 -> x5, starting transfers between devices: none -> 11.1 us  [the longest x1 3.72 us: on_device(): other = lax.ppermute(theirs, 'rep', SWAP)]
    pallas_call x0 -> x4, Pallas kernels: none -> 4.41 us  [the longest x1 2.13 us: prepare(): pl.pallas_call(prepare_kernel, in_specs=[VMEM], out_specs=ANY, out_shape=...]
    dot_general x1, matrix products: 9.86 us -> 6.25 us  [contract(): jnp.einsum('rk,jk->rj', rows, integrals[0, :, 0, :], precision=lax.Precis...]
  transfers between devices with their start and end apart: 1 -> 7, of which waited for: 1 -> 7; matrix products, arithmetic and copies ran while one was open for 0% -> 1% of each run, Pallas kernels for 0% -> 0%
where the time goes in v2:
time: 95.6 us; the launch traced here: 95.3 us
  waiting for transfers between devices  50.1 us (52%)
  starting transfers between devices  31.8 us (33%)
  matrix products  6.25 us (7%)
  Pallas kernels  4.41 us (5%)
  other arithmetic  1.94 us (2%)
    all_to_all x1, waiting for transfers between devices, on_device(): got = lax.all_to_all(outgoing, YZX, split_axis=0, concat_axis=0, tiled=True)  26 us
    all_to_all x1, starting transfers between devices, on_device(): got = lax.all_to_all(outgoing, YZX, split_axis=0, concat_axis=0, tiled=True)  16.3 us
    ppermute x3, waiting for transfers between devices, shift(): return lax.ppermute(value, axis, [(i, (i + by) % n) for i in range(n)])  11 us
    all_to_all x1, waiting for transfers between devices, on_device(): lax.all_to_all(leaving, ('y', 'z'), split_axis=0, concat_axis=0, tiled=True)  9.66 us
    dot_general x1, matrix products, contract(): jnp.einsum('rk,jk->rj', rows, integrals[0, :, 0, :], precision=lax.Precis...  6.25 us
    all_to_all x1, starting transfers between devices, on_device(): lax.all_to_all(leaving, ('y', 'z'), split_axis=0, concat_axis=0, tiled=True)  4.42 us
    ppermute x1, starting transfers between devices, on_device(): other = lax.ppermute(theirs, 'rep', SWAP)  3.72 us
    ppermute x3, starting transfers between devices, shift(): return lax.ppermute(value, axis, [(i, (i + by) % n) for i in range(n)])  3.72 us
  transfers between devices with their start and end apart: 7, of which 7 were waited for; matrix products, arithmetic and copies ran while one was open for 1% of the time, Pallas kernels for 0%

profile of v2, /device:TPU:1, one launch (start us, length us, event | category | flops | bytes accessed | tf_op | source)
XLA Modules:
  0.0 95.3 jit_solution(16244245326169317224)
XLA Ops:
  0.0 0.0 copy-start
  0.0 2.1 %prepare.1 = f32[8,4,4,2,960]{4,3,2,1,0:T(2,128)} custom-call(f32[8,2,1,3840]{3,2,1,0:T(1,128)} %amp_ref.1), custom_call_target="tpu_custom_call" | custom-call | bytes 1228800 | tf_op jit(solution)/shard_map/prepare/pallas_call | solution.py:63
  2.1 16.3 %all-to-all-start = ((f32[128,2,960]{2,1,0:T(2,128)}), f32[128,2,960]{2,1,0:T(2,128)S(1)}, u32[]{:S(2)}, u32[]{:S(2)}) async-start(f32[128,2,960]{2,1,0:T(2,128)} %bitcast.23), calls=%async_computation | async-start | bytes 2097152 | tf_op jit(solution)/shard_map/all_to_all | solution.py:184
  18.5 0.0 copy-done
  18.5 0.6 dynamic_slice.20
  19.1 0.6 fusion.5
  19.8 26.0 %all-to-all-done = f32[128,2,960]{2,1,0:T(2,128)S(1)} async-done(((f32[128,2,960]{2,1,0:T(2,128)}), f32[128,2,960]{2,1,0:T(2,128)S(1)}, u32[]{:S(2)}, u32[]{:S(2)}) %all-to-all-start) | async-done | bytes 983072 | tf_op jit(solution)/shard_map/all_to_all | solution.py:184
  45.7 0.8 arrange.1
  46.5 6.3 %fusion.2 = f32[256,1920]{1,0:T(8,128)S(1)} fusion(f32[256,960]{1,0:T(8,128)S(1)} %arrange.1, f32[1,1920,1,960]{1,3,2,0:T(8,128)} %param.4, f32[1920]{0:T(1024)S(1)} %fusion.5), kind=kOutput, calls=%fused_computation.2 | convolution fusion | flops 2831646720 | bytes 10329600 | tf_op jit(solution)/shard_map/rk,jk->rj/dot_general | solution.py:168
  52.8 1.1 %slice_select_fusion = f32[256,1024]{1,0:T(8,128)} fusion(f32[256,1920]{1,0:T(8,128)S(1)} %fusion.2, pred[]{:T(512)S(6)} %eq.8), kind=kLoop, calls=%fused_computation.4 | loop fusion | flops 262144 | bytes 3145729 | tf_op jit(solution)/shard_map/jit(_where)/select_n | solution.py:188
  53.9 3.6 %collective-permute-start = (f32[256,1024]{1,0:T(8,128)}, f32[256,1024]{1,0:T(8,128)S(1)}, u32[]{:S(2)}, u32[]{:S(2)}) collective-permute-start(f32[256,1024]{1,0:T(8,128)} %slice_select_fusion), channel_id=1, source_target_pairs={{0,1},{1,0},{2,3},{3,2},{4,5},{5,4},{6,7},{7,6},{8,9},{9,8},{10,11... | collective-permute-start | bytes 3145736 | tf_op jit(solution)/shard_map/ppermute | solution.py:188
  57.5 2.5 %collective-permute-done = f32[256,1024]{1,0:T(8,128)S(1)} collective-permute-done((f32[256,1024]{1,0:T(8,128)}, f32[256,1024]{1,0:T(8,128)S(1)}, u32[]{:S(2)}, u32[]{:S(2)}) %collective-permute-start) | collective-permute-done | bytes 1048608 | tf_op jit(solution)/shard_map/ppermute | solution.py:188
  60.0 0.2 select_add_fusion
  60.2 0.1 dynamic-slice_bitcast_fusion
  60.3 0.3 collective-permute-start.1
  60.6 2.0 %collective-permute-start.2 = (f32[64,1024]{1,0:T(8,128)S(1)}, f32[64,1024]{1,0:T(8,128)S(1)}, u32[]{:S(2)}, u32[]{:S(2)}) collective-permute-start(f32[64,1024]{1,0:T(8,128)S(1)} %get-tuple-element.6), channel_id=1, source_target_pairs={{0,4},{2,6},{4,0},{6,2},{1,5},{3,7},{5,1},{7,3},{8,12},{10,14},{12... | collective-permute-start | bytes 786440 | tf_op jit(solution)/shard_map/ppermute | solution.py:27
  62.6 1.4 %collective-permute-start.3 = (f32[64,1024]{1,0:T(8,128)S(1)}, f32[64,1024]{1,0:T(8,128)S(1)}, u32[]{:S(2)}, u32[]{:S(2)}) collective-permute-start(f32[64,1024]{1,0:T(8,128)S(1)} %get-tuple-element.5), channel_id=1, source_target_pairs={{0,6},{2,0},{4,2},{6,4},{1,7},{3,1},{5,3},{7,5},{8,14},{10,8},{12,... | collective-permute-start | bytes 786440 | tf_op jit(solution)/shard_map/ppermute | solution.py:27
  64.0 5.6 %collective-permute-done.1.refs_1_ = f32[64,1024]{1,0:T(8,128)S(1)} collective-permute-done((f32[64,1024]{1,0:T(8,128)S(1)}, f32[64,1024]{1,0:T(8,128)S(1)}, u32[]{:S(2)}, u32[]{:S(2)}) %collective-permute-start.1) | collective-permute-done | bytes 262176 | tf_op jit(solution)/shard_map/ppermute | solution.py:27
  69.6 4.7 %collective-permute-done.2.refs_2_ = f32[64,1024]{1,0:T(8,128)S(1)} collective-permute-done((f32[64,1024]{1,0:T(8,128)S(1)}, f32[64,1024]{1,0:T(8,128)S(1)}, u32[]{:S(2)}, u32[]{:S(2)}) %collective-permute-start.2) | collective-permute-done | bytes 262176 | tf_op jit(solution)/shard_map/ppermute | solution.py:27
  74.3 0.7 collective-permute-done.3.refs_3_
  75.0 0.8 gather_rows.1
  75.8 4.4 %all-to-all-start.1 = ((f32[32,2,1024]{2,1,0:T(2,128)}), f32[32,2,1024]{2,1,0:T(2,128)S(1)}, u32[]{:S(2)}, u32[]{:S(2)}) async-start(f32[32,2,1024]{2,1,0:T(2,128)} %gather_rows.1), calls=%async_computation.1 | async-start | bytes 524288 | tf_op jit(solution)/shard_map/all_to_all | solution.py:194
  80.2 9.7 %all-to-all-done.1 = f32[32,2,1024]{2,1,0:T(2,128)S(1)} async-done(((f32[32,2,1024]{2,1,0:T(2,128)}), f32[32,2,1024]{2,1,0:T(2,128)S(1)}, u32[]{:S(2)}, u32[]{:S(2)}) %all-to-all-start.1) | async-done | bytes 262176 | tf_op jit(solution)/shard_map/all_to_all | solution.py:194
  89.9 3.7 %collective-permute-start.4 = (f32[8,2,2,1024]{3,2,1,0:T(2,128)S(1)}, f32[8,2,2,1024]{3,2,1,0:T(2,128)S(1)}, u32[]{:S(2)}, u32[]{:S(2)}) collective-permute-start(f32[8,2,2,1024]{3,2,1,0:T(2,128)S(1)} %constant_dynamic-slice_fusion), channel_id=1, source_target_pairs={{0,1},{1,0},{2,3},{3,2},{4,5},{5,4},{6,7},{7,6},{8,9},{9,8},{10,11... | collective-permute-start | bytes 393224 | tf_op jit(solution)/shard_map/ppermute | solution.py:197
  93.6 1.0 %collective-permute-done.4.other_ref = f32[8,2,2,1024]{3,2,1,0:T(2,128)S(1)} collective-permute-done((f32[8,2,2,1024]{3,2,1,0:T(2,128)S(1)}, f32[8,2,2,1024]{3,2,1,0:T(2,128)S(1)}, u32[]{:S(2)}, u32[]{:S(2)}) %collective-permute-start.4) | collective-permute-done | bytes 131104 | tf_op jit(solution)/shard_map/ppermute | solution.py:197
  94.6 0.7 final_rows.1
  (1 shorter events, 0.0 us)
Async XLA Ops:
  0.0 18.5 %copy-start = (s32[8]{0:T(128)S(1)}, s32[8]{0:T(128)}, u32[]{:S(2)}) copy-start(s32[8]{0:T(128)} %count_ref.1) | copy-start | bytes 100
  2.1 43.6 %all-to-all-start = ((f32[128,2,960]{2,1,0:T(2,128)}), f32[128,2,960]{2,1,0:T(2,128)S(1)}, u32[]{:S(2)}, u32[]{:S(2)}) async-start(f32[128,2,960]{2,1,0:T(2,128)} %bitcast.23), calls=%async_computation | async-start | bytes 2097152 | tf_op jit(solution)/shard_map/all_to_all | solution.py:184
  53.9 6.1 %collective-permute-start = (f32[256,1024]{1,0:T(8,128)}, f32[256,1024]{1,0:T(8,128)S(1)}, u32[]{:S(2)}, u32[]{:S(2)}) collective-permute-start(f32[256,1024]{1,0:T(8,128)} %slice_select_fusion), channel_id=1, source_target_pairs={{0,1},{1,0},{2,3},{3,2},{4,5},{5,4},{6,7},{7,6},{8,9},{9,8},{10,11... | collective-permute-start | bytes 3145736 | tf_op jit(solution)/shard_map/ppermute | solution.py:188
  60.3 9.3 %collective-permute-start.1 = (f32[64,1024]{1,0:T(8,128)S(1)}, f32[64,1024]{1,0:T(8,128)S(1)}, u32[]{:S(2)}, u32[]{:S(2)}) collective-permute-start(f32[64,1024]{1,0:T(8,128)S(1)} %get-tuple-element.7), channel_id=1, source_target_pairs={{0,2},{2,4},{4,6},{6,0},{1,3},{3,5},{5,7},{7,1},{8,10},{10,12},{12... | collective-permute-start | bytes 786440 | tf_op jit(solution)/shard_map/ppermute | solution.py:27
  60.6 13.7 %collective-permute-start.2 = (f32[64,1024]{1,0:T(8,128)S(1)}, f32[64,1024]{1,0:T(8,128)S(1)}, u32[]{:S(2)}, u32[]{:S(2)}) collective-permute-start(f32[64,1024]{1,0:T(8,128)S(1)} %get-tuple-element.6), channel_id=1, source_target_pairs={{0,4},{2,6},{4,0},{6,2},{1,5},{3,7},{5,1},{7,3},{8,12},{10,14},{12... | collective-permute-start | bytes 786440 | tf_op jit(solution)/shard_map/ppermute | solution.py:27
  62.6 12.4 %collective-permute-start.3 = (f32[64,1024]{1,0:T(8,128)S(1)}, f32[64,1024]{1,0:T(8,128)S(1)}, u32[]{:S(2)}, u32[]{:S(2)}) collective-permute-start(f32[64,1024]{1,0:T(8,128)S(1)} %get-tuple-element.5), channel_id=1, source_target_pairs={{0,6},{2,0},{4,2},{6,4},{1,7},{3,1},{5,3},{7,5},{8,14},{10,8},{12,... | collective-permute-start | bytes 786440 | tf_op jit(solution)/shard_map/ppermute | solution.py:27
  75.8 14.1 %all-to-all-start.1 = ((f32[32,2,1024]{2,1,0:T(2,128)}), f32[32,2,1024]{2,1,0:T(2,128)S(1)}, u32[]{:S(2)}, u32[]{:S(2)}) async-start(f32[32,2,1024]{2,1,0:T(2,128)} %gather_rows.1), calls=%async_computation.1 | async-start | bytes 524288 | tf_op jit(solution)/shard_map/all_to_all | solution.py:194
  89.9 4.7 %collective-permute-start.4 = (f32[8,2,2,1024]{3,2,1,0:T(2,128)S(1)}, f32[8,2,2,1024]{3,2,1,0:T(2,128)S(1)}, u32[]{:S(2)}, u32[]{:S(2)}) collective-permute-start(f32[8,2,2,1024]{3,2,1,0:T(2,128)S(1)} %constant_dynamic-slice_fusion), channel_id=1, source_target_pairs={{0,1},{1,0},{2,3},{3,2},{4,5},{5,4},{6,7},{7,6},{8,9},{9,8},{10,11... | collective-permute-start | bytes 393224 | tf_op jit(solution)/shard_map/ppermute | solution.py:197

commit v3 on v2

--- a/solution.py
+++ b/solution.py
@@ -16,7 +16,7 @@
 LANES = 128
 PART = 1024
 STEP = 896
-CHUNKS = 1
+SPLIT_MIB = 56
 VMEM = pl.BlockSpec(memory_space=pltpu.VMEM)
 SMEM = pl.BlockSpec(memory_space=pltpu.SMEM)
 ANY = pl.BlockSpec(memory_space=pl.ANY)
@@ -75,15 +75,51 @@
     )(amplitudes)
 
 
-def arrange_kernel(count_ref, got_ref, out_ref):
+def split_kernel(count_ref, w_ref, *out_refs):
+    half = lax.axis_index("rep")
+    limit = live_limit(count_ref)
+    base = (lax.axis_index("z") % RING) * w_ref.shape[1]
+    for place, side in ((0, 1 - half), (1, half)):
+        start = pl.multiple_of(side * STEP, LANES)
+        high_ref, low_ref = out_refs[2 * place : 2 * place + 2]
+        column = base + start + lax.broadcasted_iota(jnp.int32, (1, PART), 1)
+        live = (column < limit).astype(jnp.float32)
+        w = w_ref[:, pl.ds(start, PART)] * live
+        high = w.astype(jnp.bfloat16)
+        high_ref[...] = high
+        low_ref[...] = (w - high.astype(jnp.float32)).astype(jnp.bfloat16)
+
+
+def split_tile(pair_count, tile):
+    depth, width = tile.shape
+    rows = depth // 10
+    return pl.pallas_call(
+        split_kernel,
+        grid=(10,),
+        in_specs=[SMEM, pl.BlockSpec((rows, width), lambda i: (i, 0))],
+        out_specs=[pl.BlockSpec((rows, PART), lambda i: (i, 0))] * 4,
+        out_shape=[jax.ShapeDtypeStruct((depth, PART), jnp.bfloat16)] * 4,
+        cost_estimate=cost(4 * depth * width, 8 * depth * width),
+        compiler_params=params(SPLIT_MIB),
+        name="split_tile",
+    )(pair_count, tile)
+
+
+def arrange_kernel(count_ref, got_ref, both_ref):
     width = got_ref.shape[3]
+    rows = both_ref.shape[0] // 2
     base = lax.axis_index("rep") * (RING * width) + lax.axis_index("x") * width
     slot = lax.broadcasted_iota(jnp.int32, (1, width), 1) + base
     live = (slot < live_limit(count_ref)).astype(jnp.float32)
     for x in range(RING):
         for r in range(2):
+            a = got_ref[:, x, r, :] * live
+            high = a.astype(jnp.bfloat16)
             at = (x * 2 + r) * OWNERS
-            out_ref[at : at + OWNERS, :] = got_ref[:, x, r, :] * live
+            both_ref[at : at + OWNERS, :] = high
+            both_ref[rows + at : rows + at + OWNERS, :] = (a - high.astype(jnp.float32)).astype(
+                jnp.bfloat16
+            )
 
 
 def arrange(pair_count, got):
@@ -93,22 +129,24 @@
         arrange_kernel,
         in_specs=[SMEM, VMEM],
         out_specs=VMEM,
-        out_shape=jax.ShapeDtypeStruct((rows, width), jnp.float32),
+        out_shape=jax.ShapeDtypeStruct((2 * rows, width), jnp.bfloat16),
         cost_estimate=cost(0, 8 * rows * width),
         compiler_params=params(16),
         name="arrange",
     )(pair_count, got)
 
 
-def gather_kernel(*refs):
-    out_ref = refs[-1]
-    width = PART // CHUNKS
-    for c in range(CHUNKS):
-        p = refs[c * RING : (c + 1) * RING]
-        for r in range(2):
-            at = slice(r * OWNERS, (r + 1) * OWNERS)
-            total = (p[0][at] + p[1][at]) + (p[2][at] + p[3][at])
-            out_ref[:, r, c * width : (c + 1) * width] = total
+def contract(both, high, low):
+    rows = both.shape[0] // 2
+    dims = (((1,), (0,)), ((), ()))
+    first = lax.dot_general(both, high, dims, preferred_element_type=jnp.float32)
+    second = lax.dot_general(both[:rows], low, dims, preferred_element_type=jnp.float32)
+    return first[:rows] + (first[rows:] + second)
+
+
+def gather_kernel(own_ref, left_a, right_a, left_b, right_b, out_ref):
+    out_ref[:, 0, :] = own_ref[:OWNERS] + (left_a[...] + right_a[...])
+    out_ref[:, 1, :] = own_ref[OWNERS:] + (left_b[...] + right_b[...])
 
 
 def gather(parts):
@@ -118,7 +156,7 @@
         out_specs=VMEM,
         out_shape=jax.ShapeDtypeStruct((OWNERS, 2, PART), jnp.float32),
         compiler_params=params(16),
-        cost_estimate=cost(0, 5 * 4 * OWNERS * 2 * PART),
+        cost_estimate=cost(0, 4 * 4 * OWNERS * 2 * PART),
         name="gather_rows",
     )(*parts)
 
@@ -160,37 +198,26 @@
     )(moved, other)
 
 
-def contract(rows, integrals, pair_count):
-    width = integrals.shape[1]
-    limit = pick(pair_count, lax.axis_index("y") * 2 + lax.axis_index("z") // RING)
-    column = (lax.axis_index("z") % RING) * width + lax.iota(jnp.int32, width)
-    keep = (column < limit).astype(jnp.float32)
-    partial = jnp.einsum(
-        "rk,jk->rj",
-        rows,
-        integrals[0, :, 0, :],
-        precision=lax.Precision.HIGH,
-        preferred_element_type=jnp.float32,
-    )
-    partial = partial * keep[None, :]
-    return partial[:, :PART], partial[:, STEP:]
-
-
 def on_device(amplitudes, integrals, pair_count):
     kc_width = integrals.shape[3]
     half = lax.axis_index("rep")
     my_x = lax.axis_index("x")
     outgoing = prepare(amplitudes, kc_width).reshape(-1, 2, kc_width)
     got = lax.all_to_all(outgoing, YZX, split_axis=0, concat_axis=0, tiled=True)
-    rows = arrange(pair_count, got.reshape(OWNERS, RING, 2, kc_width))
-    low, high = contract(rows, integrals, pair_count)
-    first = half == 0
-    pair_sum = jnp.where(first, low, high) + lax.ppermute(jnp.where(first, high, low), "rep", SWAP)
-    pair_sum = pair_sum.reshape(RING, 2 * OWNERS, PART)
-    parts = [pick(pair_sum, my_x)]
-    for s in range(1, RING):
-        parts.append(shift(pick(pair_sum, (my_x + s) % RING), "x", s))
-    leaving = gather(parts)
+    split = split_tile(pair_count, integrals[0, :, 0, :].T)
+    got, split = lax.optimization_barrier((got, split))
+    both = arrange(pair_count, got.reshape(OWNERS, RING, 2, kc_width))
+    arrived = lax.ppermute(contract(both, split[0], split[1]), "rep", SWAP)
+    pair_sum = contract(both, split[2], split[3]) + arrived
+    pair_sum = pair_sum.reshape(RING, 2, OWNERS, PART)
+    ours, right, across, left = [pick(pair_sum, (my_x + s) % RING) for s in range(RING)]
+    by_right = shift(across[0], "x", 1)
+    by_left = shift(across[1], "x", -1)
+    right_b = shift(right[1], "x", 1)
+    left_a = shift(left[0], "x", -1)
+    right_a = shift(right[0] + by_right, "x", 1)
+    left_b = shift(left[1] + by_left, "x", -1)
+    leaving = gather([ours.reshape(2 * OWNERS, PART), left_a, right_a, left_b, right_b])
     moved = lax.all_to_all(leaving, ("y", "z"), split_axis=0, concat_axis=0, tiled=True)
     moved = moved.reshape(NBLK, RING, 2, PART)
     theirs = lax.dynamic_slice_in_dim(moved, (1 - half) * 2, 2, axis=1)

time: 95.6 us -> 90 us (0.941)
  waiting for transfers between devices: 50.1 us -> 32.6 us
  Pallas kernels: 4.41 us -> 14.3 us
  starting transfers between devices: 31.8 us -> 35.7 us
  other arithmetic: 1.94 us -> 0.03 us
    pallas_call x0 -> x1, Pallas kernels: none -> 9.75 us  [split_tile(): pl.pallas_call(split_kernel, grid=(10,), in_specs=[SMEM, pl.BlockSpec((ro...]
    all_to_all x1, waiting for transfers between devices: 26 us -> 17.5 us  [on_device(): got = lax.all_to_all(outgoing, YZX, split_axis=0, concat_axis=0, tiled=True)]
    ppermute x3 -> x6, waiting for transfers between devices: 11 us -> 4.44 us  [shift(): return lax.ppermute(value, axis, [(i, (i + by) % n) for i in range(n)])]
    ppermute x3 -> x6, starting transfers between devices: 3.72 us -> 6.97 us  [shift(): return lax.ppermute(value, axis, [(i, (i + by) % n) for i in range(n)])]
    ppermute x1, waiting for transfers between devices: 2.5 us -> 0.01 us  [on_device(): arrived = lax.ppermute(contract(both, split[0], split[1]), 'rep', SWAP)]
    select_n x1 -> x0, other arithmetic: 1.13 us -> none  [on_device(): jnp.where(first, high, low)]
    dot_general x1 -> x4, matrix products: 6.25 us -> 5.77 us  [the longest x2 4.21 us: contract(): lax.dot_general(both, high, dims, preferred_element_type=jnp.float32)]
  transfers between devices with their start and end apart: 7 -> 10, of which waited for: 7 -> 5; matrix products, arithmetic and copies ran while one was open for 1% -> 3% of each run, Pallas kernels for 0% -> 11%
where the time goes in v3:
time: 90 us; the launch traced here: 89.5 us
  starting transfers between devices  35.7 us (40%)
  waiting for transfers between devices  32.6 us (36%)
  Pallas kernels  14.3 us (16%)
  matrix products  5.77 us (6%)
  local copies, waits for them, and re-layouts  1.01 us (1%)
    all_to_all x1, waiting for transfers between devices, on_device(): got = lax.all_to_all(outgoing, YZX, split_axis=0, concat_axis=0, tiled=True)  17.5 us
    all_to_all x1, starting transfers between devices, on_device(): got = lax.all_to_all(outgoing, YZX, split_axis=0, concat_axis=0, tiled=True)  16.3 us
    pallas_call x1, Pallas kernels, split_tile(): pl.pallas_call(split_kernel, grid=(10,), in_specs=[SMEM, pl.BlockSpec((ro...  9.75 us
    all_to_all x1, waiting for transfers between devices, on_device(): lax.all_to_all(leaving, ('y', 'z'), split_axis=0, concat_axis=0, tiled=True)  9.65 us
    ppermute x6, starting transfers between devices, shift(): return lax.ppermute(value, axis, [(i, (i + by) % n) for i in range(n)])  6.97 us
    ppermute x6, waiting for transfers between devices, shift(): return lax.ppermute(value, axis, [(i, (i + by) % n) for i in range(n)])  4.44 us
    all_to_all x1, starting transfers between devices, on_device(): lax.all_to_all(leaving, ('y', 'z'), split_axis=0, concat_axis=0, tiled=True)  4.37 us
    ppermute x1, starting transfers between devices, on_device(): other = lax.ppermute(theirs, 'rep', SWAP)  4.33 us
  transfers between devices with their start and end apart: 10, of which 5 were waited for; matrix products, arithmetic and copies ran while one was open for 3% of the time, Pallas kernels for 11%

profile of v3, /device:TPU:1, one launch (start us, length us, event | category | flops | bytes accessed | tf_op | source)
XLA Modules:
  0.0 89.5 jit_solution(17718124684870807)
XLA Ops:
  0.0 2.1 %prepare.1 = f32[8,4,4,2,960]{4,3,2,1,0:T(2,128)} custom-call(f32[8,2,1,3840]{3,2,1,0:T(1,128)} %amp_ref.1), custom_call_target="tpu_custom_call" | custom-call | bytes 1228800 | tf_op jit(solution)/shard_map/prepare/pallas_call | solution.py:63
  2.1 16.3 %all-to-all-start = ((f32[128,2,960]{2,1,0:T(2,128)}), f32[128,2,960]{2,1,0:T(2,128)S(1)}, u32[]{:S(2)}, u32[]{:S(2)}) async-start(f32[128,2,960]{2,1,0:T(2,128)} %bitcast.35), calls=%async_computation | async-start | bytes 2097152 | tf_op jit(solution)/shard_map/all_to_all | solution.py:206
  18.5 0.0 copy-start
  18.5 9.7 %split_tile.1 = (bf16[960,1024]{1,0:T(8,128)(2,1)}, bf16[960,1024]{1,0:T(8,128)(2,1)}, bf16[960,1024]{1,0:T(8,128)(2,1)}, bf16[960,1024]{1,0:T(8,128)(2,1)}) custom-call(s32[8]{0:T(128)} %count_ref.3, f32[960,1920]{1,0:T(8,128)} %bitcast.34), custom_call_target="tpu_custom_call" | custom-call | flops 7372800 | bytes 14745600 | tf_op jit(solution)/shard_map/split_tile/pallas_call | solution.py:96
  28.3 17.5 %all-to-all-done = f32[128,2,960]{2,1,0:T(2,128)S(1)} async-done(((f32[128,2,960]{2,1,0:T(2,128)}), f32[128,2,960]{2,1,0:T(2,128)S(1)}, u32[]{:S(2)}, u32[]{:S(2)}) %all-to-all-start) | async-done | bytes 983072 | tf_op jit(solution)/shard_map/all_to_all | solution.py:206
  45.7 0.9 arrange.1
  46.6 0.7 copy-done.3
  47.3 1.3 %fusion.8 = f32[512,1024]{1,0:T(8,128)S(1)} fusion(bf16[512,960]{1,0:T(8,128)(2,1)S(1)} %arrange.1, bf16[960,1024]{1,0:T(8,128)(2,1)S(1)} %copy-done.3), kind=kOutput, calls=%fused_computation.18 | convolution fusion | flops 1006632960 | bytes 5046272 | tf_op jit(solution)/shard_map/dot_general | solution.py:142
  48.6 0.3 copy-done.1
  48.8 0.7 fusion
  49.6 3.7 %collective-permute-start = (f32[256,1024]{1,0:T(8,128)S(1)}, f32[256,1024]{1,0:T(8,128)S(1)}, u32[]{:S(2)}, u32[]{:S(2)}) collective-permute-start(f32[256,1024]{1,0:T(8,128)S(1)} %fusion), channel_id=1, source_target_pairs={{0,1},{1,0},{2,3},{3,2},{4,5},{5,4},{6,7},{7,6},{8,9},{9,8},{10,11... | collective-permute-start | bytes 3145736 | tf_op jit(solution)/shard_map/ppermute | solution.py:210
  53.3 2.9 %fusion.7 = f32[512,1024]{1,0:T(8,128)S(1)} fusion(bf16[512,960]{1,0:T(8,128)(2,1)S(1)} %arrange.1, bf16[960,1024]{1,0:T(8,128)(2,1)} %get-tuple-element.19), kind=kOutput, calls=%fused_computation.17 | convolution fusion | flops 1006632960 | bytes 5046272 | tf_op jit(solution)/shard_map/dot_general | solution.py:142
  56.2 0.0 collective-permute-done
  56.3 0.8 fusion.2
  57.1 0.1 dynamic-slice_bitcast_fusion
  57.1 0.3 collective-permute-start.2
  57.5 2.4 %collective-permute-start.4 = (f32[32,1024]{1,0:T(8,128)S(1)}, f32[32,1024]{1,0:T(8,128)S(1)}, u32[]{:S(2)}, u32[]{:S(2)}) collective-permute-start(f32[32,1024]{1,0:T(8,128)S(1)} %get-tuple-element.26), channel_id=1, source_target_pairs={{0,6},{2,0},{4,2},{6,4},{1,7},{3,1},{5,3},{7,5},{8,14},{10,8},{12,... | collective-permute-start | bytes 393224 | tf_op jit(solution)/shard_map/ppermute | solution.py:27
  59.9 0.0 collective-permute-start.1
  59.9 1.4 %collective-permute-start.6 = (f32[32,1024]{1,0:T(8,128)S(1)}, f32[32,1024]{1,0:T(8,128)S(1)}, u32[]{:S(2)}, u32[]{:S(2)}) collective-permute-start(f32[32,1024]{1,0:T(8,128)S(1)} %get-tuple-element.23), channel_id=1, source_target_pairs={{0,2},{2,4},{4,6},{6,0},{1,3},{3,5},{5,7},{7,1},{8,10},{10,12},{12... | collective-permute-start | bytes 393224 | tf_op jit(solution)/shard_map/ppermute | solution.py:27
  61.4 2.1 %collective-permute-done.2 = f32[32,1024]{1,0:T(8,128)S(1)} collective-permute-done((f32[32,1024]{1,0:T(8,128)S(1)}, f32[32,1024]{1,0:T(8,128)S(1)}, u32[]{:S(2)}, u32[]{:S(2)}) %collective-permute-start.2) | collective-permute-done | bytes 131104 | tf_op jit(solution)/shard_map/ppermute | solution.py:27
  63.5 0.0 collective-permute-done.4
  63.5 0.1 collective-permute-start.3
  63.6 2.7 %collective-permute-start.5 = (f32[32,1024]{1,0:T(8,128)S(1)}, f32[32,1024]{1,0:T(8,128)S(1)}, u32[]{:S(2)}, u32[]{:S(2)}) collective-permute-start(f32[32,1024]{1,0:T(8,128)S(1)} %get-tuple-element.27), channel_id=1, source_target_pairs={{0,6},{2,0},{4,2},{6,4},{1,7},{3,1},{5,3},{7,5},{8,14},{10,8},{12,... | collective-permute-start | bytes 393224 | tf_op jit(solution)/shard_map/ppermute | solution.py:27
  66.3 0.0 collective-permute-done.1.left_a
  66.3 0.0 collective-permute-done.6.right_b
  66.3 2.3 %collective-permute-done.3.right_a = f32[32,1024]{1,0:T(8,128)S(1)} collective-permute-done((f32[32,1024]{1,0:T(8,128)S(1)}, f32[32,1024]{1,0:T(8,128)S(1)}, u32[]{:S(2)}, u32[]{:S(2)}) %collective-permute-start.3) | collective-permute-done | bytes 131104 | tf_op jit(solution)/shard_map/ppermute | solution.py:27
  68.6 0.8 gather_rows.1
  69.4 4.4 %all-to-all-start.1 = ((f32[32,2,1024]{2,1,0:T(2,128)}), f32[32,2,1024]{2,1,0:T(2,128)S(1)}, u32[]{:S(2)}, u32[]{:S(2)}) async-start(f32[32,2,1024]{2,1,0:T(2,128)} %gather_rows.1), calls=%async_computation.1 | async-start | bytes 524288 | tf_op jit(solution)/shard_map/all_to_all | solution.py:221
  73.8 9.7 %all-to-all-done.1 = f32[32,2,1024]{2,1,0:T(2,128)S(1)} async-done(((f32[32,2,1024]{2,1,0:T(2,128)}), f32[32,2,1024]{2,1,0:T(2,128)S(1)}, u32[]{:S(2)}, u32[]{:S(2)}) %all-to-all-start.1) | async-done | bytes 262176 | tf_op jit(solution)/shard_map/all_to_all | solution.py:221
  83.5 4.3 %collective-permute-start.7 = (f32[8,2,2,1024]{3,2,1,0:T(2,128)S(1)}, f32[8,2,2,1024]{3,2,1,0:T(2,128)S(1)}, u32[]{:S(2)}, u32[]{:S(2)}) collective-permute-start(f32[8,2,2,1024]{3,2,1,0:T(2,128)S(1)} %constant_dynamic-slice_fusion), channel_id=1, source_target_pairs={{0,1},{1,0},{2,3},{3,2},{4,5},{5,4},{6,7},{7,6},{8,9},{9,8},{10,11... | collective-permute-start | bytes 393224 | tf_op jit(solution)/shard_map/ppermute | solution.py:224
  87.8 1.0 %collective-permute-done.7.other_ref = f32[8,2,2,1024]{3,2,1,0:T(2,128)S(1)} collective-permute-done((f32[8,2,2,1024]{3,2,1,0:T(2,128)S(1)}, f32[8,2,2,1024]{3,2,1,0:T(2,128)S(1)}, u32[]{:S(2)}, u32[]{:S(2)}) %collective-permute-start.7) | collective-permute-done | bytes 131104 | tf_op jit(solution)/shard_map/ppermute | solution.py:224
  88.8 0.7 final_rows.1
  (9 shorter events, 0.1 us)
Async XLA Ops:
  2.1 43.6 %all-to-all-start = ((f32[128,2,960]{2,1,0:T(2,128)}), f32[128,2,960]{2,1,0:T(2,128)S(1)}, u32[]{:S(2)}, u32[]{:S(2)}) async-start(f32[128,2,960]{2,1,0:T(2,128)} %bitcast.35), calls=%async_computation | async-start | bytes 2097152 | tf_op jit(solution)/shard_map/all_to_all | solution.py:206
  18.5 27.2 %copy-start = (s32[8]{0:T(128)S(1)}, s32[8]{0:T(128)}, u32[]{:S(2)}) copy-start(s32[8]{0:T(128)} %count_ref.3) | copy-start | bytes 100
  45.7 1.5 %copy-start.3 = (bf16[960,1024]{1,0:T(8,128)(2,1)S(1)}, bf16[960,1024]{1,0:T(8,128)(2,1)}, u32[]{:S(2)}) copy-start(bf16[960,1024]{1,0:T(8,128)(2,1)} %get-tuple-element.21) | copy-start | bytes 5898244
  47.3 1.5 %copy-start.1 = (bf16[960,1024]{1,0:T(8,128)(2,1)S(1)}, bf16[960,1024]{1,0:T(8,128)(2,1)}, u32[]{:S(2)}) copy-start(bf16[960,1024]{1,0:T(8,128)(2,1)} %get-tuple-element.22) | copy-start | bytes 5898244
  49.6 6.7 %collective-permute-start = (f32[256,1024]{1,0:T(8,128)S(1)}, f32[256,1024]{1,0:T(8,128)S(1)}, u32[]{:S(2)}, u32[]{:S(2)}) collective-permute-start(f32[256,1024]{1,0:T(8,128)S(1)} %fusion), channel_id=1, source_target_pairs={{0,1},{1,0},{2,3},{3,2},{4,5},{5,4},{6,7},{7,6},{8,9},{9,8},{10,11... | collective-permute-start | bytes 3145736 | tf_op jit(solution)/shard_map/ppermute | solution.py:210
  53.3 3.0 %copy-start.2 = (bf16[960,1024]{1,0:T(8,128)(2,1)S(1)}, bf16[960,1024]{1,0:T(8,128)(2,1)}, u32[]{:S(2)}) copy-start(bf16[960,1024]{1,0:T(8,128)(2,1)} %get-tuple-element.20) | copy-start | bytes 5898244
  57.1 6.3 %collective-permute-start.2 = (f32[32,1024]{1,0:T(8,128)S(1)}, f32[32,1024]{1,0:T(8,128)S(1)}, u32[]{:S(2)}, u32[]{:S(2)}) collective-permute-start(f32[32,1024]{1,0:T(8,128)S(1)} %get-tuple-element.24), channel_id=1, source_target_pairs={{0,2},{2,4},{4,6},{6,0},{1,3},{3,5},{5,7},{7,1},{8,10},{10,12},{12... | collective-permute-start | bytes 393224 | tf_op jit(solution)/shard_map/ppermute | solution.py:27
  57.5 6.0 %collective-permute-start.4 = (f32[32,1024]{1,0:T(8,128)S(1)}, f32[32,1024]{1,0:T(8,128)S(1)}, u32[]{:S(2)}, u32[]{:S(2)}) collective-permute-start(f32[32,1024]{1,0:T(8,128)S(1)} %get-tuple-element.26), channel_id=1, source_target_pairs={{0,6},{2,0},{4,2},{6,4},{1,7},{3,1},{5,3},{7,5},{8,14},{10,8},{12,... | collective-permute-start | bytes 393224 | tf_op jit(solution)/shard_map/ppermute | solution.py:27
  59.9 6.4 %collective-permute-start.1 = (f32[32,1024]{1,0:T(8,128)S(1)}, f32[32,1024]{1,0:T(8,128)S(1)}, u32[]{:S(2)}, u32[]{:S(2)}) collective-permute-start(f32[32,1024]{1,0:T(8,128)S(1)} %get-tuple-element.25), channel_id=1, source_target_pairs={{0,6},{2,0},{4,2},{6,4},{1,7},{3,1},{5,3},{7,5},{8,14},{10,8},{12,... | collective-permute-start | bytes 393224 | tf_op jit(solution)/shard_map/ppermute | solution.py:27
  59.9 6.4 %collective-permute-start.6 = (f32[32,1024]{1,0:T(8,128)S(1)}, f32[32,1024]{1,0:T(8,128)S(1)}, u32[]{:S(2)}, u32[]{:S(2)}) collective-permute-start(f32[32,1024]{1,0:T(8,128)S(1)} %get-tuple-element.23), channel_id=1, source_target_pairs={{0,2},{2,4},{4,6},{6,0},{1,3},{3,5},{5,7},{7,1},{8,10},{10,12},{12... | collective-permute-start | bytes 393224 | tf_op jit(solution)/shard_map/ppermute | solution.py:27
  63.5 5.1 %collective-permute-start.3 = (f32[32,1024]{1,0:T(8,128)S(1)}, f32[32,1024]{1,0:T(8,128)S(1)}, u32[]{:S(2)}, u32[]{:S(2)}) collective-permute-start(f32[32,1024]{1,0:T(8,128)S(1)} %get-tuple-element.28), channel_id=1, source_target_pairs={{0,2},{2,4},{4,6},{6,0},{1,3},{3,5},{5,7},{7,1},{8,10},{10,12},{12... | collective-permute-start | bytes 393224 | tf_op jit(solution)/shard_map/ppermute | solution.py:27
  63.6 5.0 %collective-permute-start.5 = (f32[32,1024]{1,0:T(8,128)S(1)}, f32[32,1024]{1,0:T(8,128)S(1)}, u32[]{:S(2)}, u32[]{:S(2)}) collective-permute-start(f32[32,1024]{1,0:T(8,128)S(1)} %get-tuple-element.27), channel_id=1, source_target_pairs={{0,6},{2,0},{4,2},{6,4},{1,7},{3,1},{5,3},{7,5},{8,14},{10,8},{12,... | collective-permute-start | bytes 393224 | tf_op jit(solution)/shard_map/ppermute | solution.py:27
  69.4 14.0 %all-to-all-start.1 = ((f32[32,2,1024]{2,1,0:T(2,128)}), f32[32,2,1024]{2,1,0:T(2,128)S(1)}, u32[]{:S(2)}, u32[]{:S(2)}) async-start(f32[32,2,1024]{2,1,0:T(2,128)} %gather_rows.1), calls=%async_computation.1 | async-start | bytes 524288 | tf_op jit(solution)/shard_map/all_to_all | solution.py:221
  83.5 5.3 %collective-permute-start.7 = (f32[8,2,2,1024]{3,2,1,0:T(2,128)S(1)}, f32[8,2,2,1024]{3,2,1,0:T(2,128)S(1)}, u32[]{:S(2)}, u32[]{:S(2)}) collective-permute-start(f32[8,2,2,1024]{3,2,1,0:T(2,128)S(1)} %constant_dynamic-slice_fusion), channel_id=1, source_target_pairs={{0,1},{1,0},{2,3},{3,2},{4,5},{5,4},{6,7},{7,6},{8,9},{9,8},{10,11... | collective-permute-start | bytes 393224 | tf_op jit(solution)/shard_map/ppermute | solution.py:224

commit v4 on v3

--- a/solution.py
+++ b/solution.py
@@ -44,12 +44,13 @@
 
 
 def prepare_kernel(amp_ref, out_hbm, piece_ref, sems):
-    width = piece_ref.shape[3]
+    width = piece_ref.shape[3] // 2
     for g in range(NBLK):
-        for r in range(2):
-            row = amp_ref[g, r]
-            for k in range(RING):
-                piece_ref[g, k, r : r + 1, :] = row[:, k * width : (k + 1) * width]
+        for k in range(RING):
+            for r in range(2):
+                piece_ref[g, k, :, r * width : (r + 1) * width] = amp_ref[g, r][
+                    :, k * width : (k + 1) * width
+                ]
     copies = [
         pltpu.make_async_copy(piece_ref, out_hbm.at[:, j], sems.at[j]) for j in range(RING)
     ]
@@ -64,9 +65,9 @@
         prepare_kernel,
         in_specs=[VMEM],
         out_specs=ANY,
-        out_shape=jax.ShapeDtypeStruct((NBLK, RING, RING, 2, width), jnp.float32),
+        out_shape=jax.ShapeDtypeStruct((NBLK, RING, RING, 1, 2 * width), jnp.float32),
         scratch_shapes=[
-            pltpu.VMEM((NBLK, RING, 2, width), jnp.float32),
+            pltpu.VMEM((NBLK, RING, 1, 2 * width), jnp.float32),
             pltpu.SemaphoreType.DMA((RING,)),
         ],
         cost_estimate=cost(0, 5 * 4 * amplitudes.size),
@@ -106,14 +107,14 @@
 
 
 def arrange_kernel(count_ref, got_ref, both_ref):
-    width = got_ref.shape[3]
+    width = got_ref.shape[3] // 2
     rows = both_ref.shape[0] // 2
     base = lax.axis_index("rep") * (RING * width) + lax.axis_index("x") * width
     slot = lax.broadcasted_iota(jnp.int32, (1, width), 1) + base
     live = (slot < live_limit(count_ref)).astype(jnp.float32)
     for x in range(RING):
         for r in range(2):
-            a = got_ref[:, x, r, :] * live
+            a = got_ref[:, x, 0, r * width : (r + 1) * width] * live
             high = a.astype(jnp.bfloat16)
             at = (x * 2 + r) * OWNERS
             both_ref[at : at + OWNERS, :] = high
@@ -123,7 +124,7 @@
 
 
 def arrange(pair_count, got):
-    width = got.shape[3]
+    width = got.shape[3] // 2
     rows = OWNERS * RING * 2
     return pl.pallas_call(
         arrange_kernel,
@@ -202,11 +203,11 @@
     kc_width = integrals.shape[3]
     half = lax.axis_index("rep")
     my_x = lax.axis_index("x")
-    outgoing = prepare(amplitudes, kc_width).reshape(-1, 2, kc_width)
+    outgoing = prepare(amplitudes, kc_width).reshape(-1, 1, 2 * kc_width)
     got = lax.all_to_all(outgoing, YZX, split_axis=0, concat_axis=0, tiled=True)
     split = split_tile(pair_count, integrals[0, :, 0, :].T)
     got, split = lax.optimization_barrier((got, split))
-    both = arrange(pair_count, got.reshape(OWNERS, RING, 2, kc_width))
+    both = arrange(pair_count, got.reshape(OWNERS, RING, 1, 2 * kc_width))
     arrived = lax.ppermute(contract(both, split[0], split[1]), "rep", SWAP)
     pair_sum = contract(both, split[2], split[3]) + arrived
     pair_sum = pair_sum.reshape(RING, 2, OWNERS, PART)

time: 90 us -> 88.6 us (0.984)
  waiting for transfers between devices: 32.6 us -> 31.2 us
    all_to_all x1, waiting for transfers between devices: 17.5 us -> 16.1 us  [on_device(): got = lax.all_to_all(outgoing, YZX, split_axis=0, concat_axis=0, tiled=True)]
where the time goes in v4:
time: 88.6 us; the launch traced here: 88.1 us
  starting transfers between devices  35.7 us (40%)
  waiting for transfers between devices  31.2 us (35%)
  Pallas kernels  14.3 us (16%)
  matrix products  5.77 us (7%)
  local copies, waits for them, and re-layouts  0.97 us (1%)
    all_to_all x1, starting transfers between devices, on_device(): got = lax.all_to_all(outgoing, YZX, split_axis=0, concat_axis=0, tiled=True)  16.3 us
    all_to_all x1, waiting for transfers between devices, on_device(): got = lax.all_to_all(outgoing, YZX, split_axis=0, concat_axis=0, tiled=True)  16.1 us
    pallas_call x1, Pallas kernels, split_tile(): pl.pallas_call(split_kernel, grid=(10,), in_specs=[SMEM, pl.BlockSpec((ro...  9.75 us
    all_to_all x1, waiting for transfers between devices, on_device(): lax.all_to_all(leaving, ('y', 'z'), split_axis=0, concat_axis=0, tiled=True)  9.65 us
    ppermute x6, starting transfers between devices, shift(): return lax.ppermute(value, axis, [(i, (i + by) % n) for i in range(n)])  6.97 us
    ppermute x6, waiting for transfers between devices, shift(): return lax.ppermute(value, axis, [(i, (i + by) % n) for i in range(n)])  4.44 us
    ppermute x1, starting transfers between devices, on_device(): other = lax.ppermute(theirs, 'rep', SWAP)  4.33 us
    all_to_all x1, starting transfers between devices, on_device(): lax.all_to_all(leaving, ('y', 'z'), split_axis=0, concat_axis=0, tiled=True)  4.27 us
  transfers between devices with their start and end apart: 10, of which 5 were waited for; matrix products, arithmetic and copies ran while one was open for 3% of the time, Pallas kernels for 11%

profile of v4, /device:TPU:1, one launch (start us, length us, event | category | flops | bytes accessed | tf_op | source)
XLA Modules:
  0.0 88.1 jit_solution(14815864006523978815)
XLA Ops:
  0.0 2.2 %prepare.1 = f32[8,4,4,1,1920]{4,3,2,1,0:T(1,128)} custom-call(f32[8,2,1,3840]{3,2,1,0:T(1,128)} %amp_ref.1), custom_call_target="tpu_custom_call" | custom-call | bytes 1228800 | tf_op jit(solution)/shard_map/prepare/pallas_call | solution.py:64
  2.2 16.3 %all-to-all-start = ((f32[128,1,1920]{2,1,0:T(1,128)}), f32[128,1,1920]{2,1,0:T(1,128)S(1)}, u32[]{:S(2)}, u32[]{:S(2)}) async-start(f32[128,1,1920]{2,1,0:T(1,128)} %bitcast.38), calls=%async_computation | async-start | bytes 1966080 | tf_op jit(solution)/shard_map/all_to_all | solution.py:207
  18.5 0.0 copy-start
  18.5 9.7 %split_tile.1 = (bf16[960,1024]{1,0:T(8,128)(2,1)}, bf16[960,1024]{1,0:T(8,128)(2,1)}, bf16[960,1024]{1,0:T(8,128)(2,1)}, bf16[960,1024]{1,0:T(8,128)(2,1)}) custom-call(s32[8]{0:T(128)} %count_ref.3, f32[960,1920]{1,0:T(8,128)} %bitcast.34), custom_call_target="tpu_custom_call" | custom-call | flops 7372800 | bytes 14745600 | tf_op jit(solution)/shard_map/split_tile/pallas_call | solution.py:97
  28.3 16.1 %all-to-all-done = f32[128,1,1920]{2,1,0:T(1,128)S(1)} async-done(((f32[128,1,1920]{2,1,0:T(1,128)}), f32[128,1,1920]{2,1,0:T(1,128)S(1)}, u32[]{:S(2)}, u32[]{:S(2)}) %all-to-all-start) | async-done | bytes 983072 | tf_op jit(solution)/shard_map/all_to_all | solution.py:207
  44.4 0.9 %arrange.1 = bf16[512,960]{1,0:T(8,128)(2,1)S(1)} custom-call(s32[8]{0:T(128)S(1)} %copy-done, f32[32,4,1,1920]{3,2,1,0:T(1,128)S(1)} %bitcast.30), custom_call_target="tpu_custom_call" | custom-call | bytes 1966080 | tf_op jit(solution)/shard_map/arrange/pallas_call | solution.py:129
  45.3 0.6 copy-done.3
  45.9 1.3 %fusion.8 = f32[512,1024]{1,0:T(8,128)S(1)} fusion(bf16[512,960]{1,0:T(8,128)(2,1)S(1)} %arrange.1, bf16[960,1024]{1,0:T(8,128)(2,1)S(1)} %copy-done.3), kind=kOutput, calls=%fused_computation.18 | convolution fusion | flops 1006632960 | bytes 5046272 | tf_op jit(solution)/shard_map/dot_general | solution.py:143
  47.2 0.3 copy-done.1
  47.5 0.7 fusion
  48.2 3.8 %collective-permute-start = (f32[256,1024]{1,0:T(8,128)S(1)}, f32[256,1024]{1,0:T(8,128)S(1)}, u32[]{:S(2)}, u32[]{:S(2)}) collective-permute-start(f32[256,1024]{1,0:T(8,128)S(1)} %fusion), channel_id=1, source_target_pairs={{0,1},{1,0},{2,3},{3,2},{4,5},{5,4},{6,7},{7,6},{8,9},{9,8},{10,11... | collective-permute-start | bytes 3145736 | tf_op jit(solution)/shard_map/ppermute | solution.py:211
  52.0 2.9 %fusion.7 = f32[512,1024]{1,0:T(8,128)S(1)} fusion(bf16[512,960]{1,0:T(8,128)(2,1)S(1)} %arrange.1, bf16[960,1024]{1,0:T(8,128)(2,1)} %get-tuple-element.19), kind=kOutput, calls=%fused_computation.17 | convolution fusion | flops 1006632960 | bytes 5046272 | tf_op jit(solution)/shard_map/dot_general | solution.py:143
  55.0 0.0 collective-permute-done
  55.0 0.8 fusion.2
  55.8 0.1 dynamic-slice_bitcast_fusion
  55.9 0.2 collective-permute-start.2
  56.1 2.5 %collective-permute-start.4 = (f32[32,1024]{1,0:T(8,128)S(1)}, f32[32,1024]{1,0:T(8,128)S(1)}, u32[]{:S(2)}, u32[]{:S(2)}) collective-permute-start(f32[32,1024]{1,0:T(8,128)S(1)} %get-tuple-element.26), channel_id=1, source_target_pairs={{0,6},{2,0},{4,2},{6,4},{1,7},{3,1},{5,3},{7,5},{8,14},{10,8},{12,... | collective-permute-start | bytes 393224 | tf_op jit(solution)/shard_map/ppermute | solution.py:27
  58.6 0.0 collective-permute-start.1
  58.7 1.4 %collective-permute-start.6 = (f32[32,1024]{1,0:T(8,128)S(1)}, f32[32,1024]{1,0:T(8,128)S(1)}, u32[]{:S(2)}, u32[]{:S(2)}) collective-permute-start(f32[32,1024]{1,0:T(8,128)S(1)} %get-tuple-element.23), channel_id=1, source_target_pairs={{0,2},{2,4},{4,6},{6,0},{1,3},{3,5},{5,7},{7,1},{8,10},{10,12},{12... | collective-permute-start | bytes 393224 | tf_op jit(solution)/shard_map/ppermute | solution.py:27
  60.1 2.1 %collective-permute-done.2 = f32[32,1024]{1,0:T(8,128)S(1)} collective-permute-done((f32[32,1024]{1,0:T(8,128)S(1)}, f32[32,1024]{1,0:T(8,128)S(1)}, u32[]{:S(2)}, u32[]{:S(2)}) %collective-permute-start.2) | collective-permute-done | bytes 131104 | tf_op jit(solution)/shard_map/ppermute | solution.py:27
  62.2 0.0 collective-permute-done.4
  62.2 0.1 collective-permute-start.3
  62.3 2.7 %collective-permute-start.5 = (f32[32,1024]{1,0:T(8,128)S(1)}, f32[32,1024]{1,0:T(8,128)S(1)}, u32[]{:S(2)}, u32[]{:S(2)}) collective-permute-start(f32[32,1024]{1,0:T(8,128)S(1)} %get-tuple-element.27), channel_id=1, source_target_pairs={{0,6},{2,0},{4,2},{6,4},{1,7},{3,1},{5,3},{7,5},{8,14},{10,8},{12,... | collective-permute-start | bytes 393224 | tf_op jit(solution)/shard_map/ppermute | solution.py:27
  65.0 0.0 collective-permute-done.1.left_a
  65.0 0.0 collective-permute-done.6.right_b
  65.0 2.3 %collective-permute-done.3.right_a = f32[32,1024]{1,0:T(8,128)S(1)} collective-permute-done((f32[32,1024]{1,0:T(8,128)S(1)}, f32[32,1024]{1,0:T(8,128)S(1)}, u32[]{:S(2)}, u32[]{:S(2)}) %collective-permute-start.3) | collective-permute-done | bytes 131104 | tf_op jit(solution)/shard_map/ppermute | solution.py:27
  67.4 0.8 gather_rows.1
  68.1 4.3 %all-to-all-start.1 = ((f32[32,2,1024]{2,1,0:T(2,128)}), f32[32,2,1024]{2,1,0:T(2,128)S(1)}, u32[]{:S(2)}, u32[]{:S(2)}) async-start(f32[32,2,1024]{2,1,0:T(2,128)} %gather_rows.1), calls=%async_computation.1 | async-start | bytes 524288 | tf_op jit(solution)/shard_map/all_to_all | solution.py:222
  72.4 9.7 %all-to-all-done.1 = f32[32,2,1024]{2,1,0:T(2,128)S(1)} async-done(((f32[32,2,1024]{2,1,0:T(2,128)}), f32[32,2,1024]{2,1,0:T(2,128)S(1)}, u32[]{:S(2)}, u32[]{:S(2)}) %all-to-all-start.1) | async-done | bytes 262176 | tf_op jit(solution)/shard_map/all_to_all | solution.py:222
  82.1 4.3 %collective-permute-start.7 = (f32[8,2,2,1024]{3,2,1,0:T(2,128)S(1)}, f32[8,2,2,1024]{3,2,1,0:T(2,128)S(1)}, u32[]{:S(2)}, u32[]{:S(2)}) collective-permute-start(f32[8,2,2,1024]{3,2,1,0:T(2,128)S(1)} %constant_dynamic-slice_fusion), channel_id=1, source_target_pairs={{0,1},{1,0},{2,3},{3,2},{4,5},{5,4},{6,7},{7,6},{8,9},{9,8},{10,11... | collective-permute-start | bytes 393224 | tf_op jit(solution)/shard_map/ppermute | solution.py:225
  86.4 1.0 %collective-permute-done.7.other_ref = f32[8,2,2,1024]{3,2,1,0:T(2,128)S(1)} collective-permute-done((f32[8,2,2,1024]{3,2,1,0:T(2,128)S(1)}, f32[8,2,2,1024]{3,2,1,0:T(2,128)S(1)}, u32[]{:S(2)}, u32[]{:S(2)}) %collective-permute-start.7) | collective-permute-done | bytes 131104 | tf_op jit(solution)/shard_map/ppermute | solution.py:225
  87.4 0.7 final_rows.1
  (9 shorter events, 0.1 us)
Async XLA Ops:
  2.2 42.2 %all-to-all-start = ((f32[128,1,1920]{2,1,0:T(1,128)}), f32[128,1,1920]{2,1,0:T(1,128)S(1)}, u32[]{:S(2)}, u32[]{:S(2)}) async-start(f32[128,1,1920]{2,1,0:T(1,128)} %bitcast.38), calls=%async_computation | async-start | bytes 1966080 | tf_op jit(solution)/shard_map/all_to_all | solution.py:207
  18.5 25.9 %copy-start = (s32[8]{0:T(128)S(1)}, s32[8]{0:T(128)}, u32[]{:S(2)}) copy-start(s32[8]{0:T(128)} %count_ref.3) | copy-start | bytes 100
  44.4 1.5 %copy-start.3 = (bf16[960,1024]{1,0:T(8,128)(2,1)S(1)}, bf16[960,1024]{1,0:T(8,128)(2,1)}, u32[]{:S(2)}) copy-start(bf16[960,1024]{1,0:T(8,128)(2,1)} %get-tuple-element.21) | copy-start | bytes 5898244
  45.9 1.5 %copy-start.1 = (bf16[960,1024]{1,0:T(8,128)(2,1)S(1)}, bf16[960,1024]{1,0:T(8,128)(2,1)}, u32[]{:S(2)}) copy-start(bf16[960,1024]{1,0:T(8,128)(2,1)} %get-tuple-element.22) | copy-start | bytes 5898244
  48.2 6.7 %collective-permute-start = (f32[256,1024]{1,0:T(8,128)S(1)}, f32[256,1024]{1,0:T(8,128)S(1)}, u32[]{:S(2)}, u32[]{:S(2)}) collective-permute-start(f32[256,1024]{1,0:T(8,128)S(1)} %fusion), channel_id=1, source_target_pairs={{0,1},{1,0},{2,3},{3,2},{4,5},{5,4},{6,7},{7,6},{8,9},{9,8},{10,11... | collective-permute-start | bytes 3145736 | tf_op jit(solution)/shard_map/ppermute | solution.py:211
  52.0 3.0 %copy-start.2 = (bf16[960,1024]{1,0:T(8,128)(2,1)S(1)}, bf16[960,1024]{1,0:T(8,128)(2,1)}, u32[]{:S(2)}) copy-start(bf16[960,1024]{1,0:T(8,128)(2,1)} %get-tuple-element.20) | copy-start | bytes 5898244
  55.9 6.3 %collective-permute-start.2 = (f32[32,1024]{1,0:T(8,128)S(1)}, f32[32,1024]{1,0:T(8,128)S(1)}, u32[]{:S(2)}, u32[]{:S(2)}) collective-permute-start(f32[32,1024]{1,0:T(8,128)S(1)} %get-tuple-element.24), channel_id=1, source_target_pairs={{0,2},{2,4},{4,6},{6,0},{1,3},{3,5},{5,7},{7,1},{8,10},{10,12},{12... | collective-permute-start | bytes 393224 | tf_op jit(solution)/shard_map/ppermute | solution.py:27
  56.1 6.1 %collective-permute-start.4 = (f32[32,1024]{1,0:T(8,128)S(1)}, f32[32,1024]{1,0:T(8,128)S(1)}, u32[]{:S(2)}, u32[]{:S(2)}) collective-permute-start(f32[32,1024]{1,0:T(8,128)S(1)} %get-tuple-element.26), channel_id=1, source_target_pairs={{0,6},{2,0},{4,2},{6,4},{1,7},{3,1},{5,3},{7,5},{8,14},{10,8},{12,... | collective-permute-start | bytes 393224 | tf_op jit(solution)/shard_map/ppermute | solution.py:27
  58.6 6.4 %collective-permute-start.1 = (f32[32,1024]{1,0:T(8,128)S(1)}, f32[32,1024]{1,0:T(8,128)S(1)}, u32[]{:S(2)}, u32[]{:S(2)}) collective-permute-start(f32[32,1024]{1,0:T(8,128)S(1)} %get-tuple-element.25), channel_id=1, source_target_pairs={{0,6},{2,0},{4,2},{6,4},{1,7},{3,1},{5,3},{7,5},{8,14},{10,8},{12,... | collective-permute-start | bytes 393224 | tf_op jit(solution)/shard_map/ppermute | solution.py:27
  58.7 6.4 %collective-permute-start.6 = (f32[32,1024]{1,0:T(8,128)S(1)}, f32[32,1024]{1,0:T(8,128)S(1)}, u32[]{:S(2)}, u32[]{:S(2)}) collective-permute-start(f32[32,1024]{1,0:T(8,128)S(1)} %get-tuple-element.23), channel_id=1, source_target_pairs={{0,2},{2,4},{4,6},{6,0},{1,3},{3,5},{5,7},{7,1},{8,10},{10,12},{12... | collective-permute-start | bytes 393224 | tf_op jit(solution)/shard_map/ppermute | solution.py:27
  62.2 5.1 %collective-permute-start.3 = (f32[32,1024]{1,0:T(8,128)S(1)}, f32[32,1024]{1,0:T(8,128)S(1)}, u32[]{:S(2)}, u32[]{:S(2)}) collective-permute-start(f32[32,1024]{1,0:T(8,128)S(1)} %get-tuple-element.28), channel_id=1, source_target_pairs={{0,2},{2,4},{4,6},{6,0},{1,3},{3,5},{5,7},{7,1},{8,10},{10,12},{12... | collective-permute-start | bytes 393224 | tf_op jit(solution)/shard_map/ppermute | solution.py:27
  62.3 5.0 %collective-permute-start.5 = (f32[32,1024]{1,0:T(8,128)S(1)}, f32[32,1024]{1,0:T(8,128)S(1)}, u32[]{:S(2)}, u32[]{:S(2)}) collective-permute-start(f32[32,1024]{1,0:T(8,128)S(1)} %get-tuple-element.27), channel_id=1, source_target_pairs={{0,6},{2,0},{4,2},{6,4},{1,7},{3,1},{5,3},{7,5},{8,14},{10,8},{12,... | collective-permute-start | bytes 393224 | tf_op jit(solution)/shard_map/ppermute | solution.py:27
  68.1 13.9 %all-to-all-start.1 = ((f32[32,2,1024]{2,1,0:T(2,128)}), f32[32,2,1024]{2,1,0:T(2,128)S(1)}, u32[]{:S(2)}, u32[]{:S(2)}) async-start(f32[32,2,1024]{2,1,0:T(2,128)} %gather_rows.1), calls=%async_computation.1 | async-start | bytes 524288 | tf_op jit(solution)/shard_map/all_to_all | solution.py:222
  82.1 5.3 %collective-permute-start.7 = (f32[8,2,2,1024]{3,2,1,0:T(2,128)S(1)}, f32[8,2,2,1024]{3,2,1,0:T(2,128)S(1)}, u32[]{:S(2)}, u32[]{:S(2)}) collective-permute-start(f32[8,2,2,1024]{3,2,1,0:T(2,128)S(1)} %constant_dynamic-slice_fusion), channel_id=1, source_target_pairs={{0,1},{1,0},{2,3},{3,2},{4,5},{5,4},{6,7},{7,6},{8,9},{9,8},{10,11... | collective-permute-start | bytes 393224 | tf_op jit(solution)/shard_map/ppermute | solution.py:225

commit v5 on v4

--- a/solution.py
+++ b/solution.py
@@ -17,6 +17,7 @@
 PART = 1024
 STEP = 896
 SPLIT_MIB = 56
+PARTS = 2
 VMEM = pl.BlockSpec(memory_space=pltpu.VMEM)
 SMEM = pl.BlockSpec(memory_space=pltpu.SMEM)
 ANY = pl.BlockSpec(memory_space=pl.ANY)
@@ -44,31 +45,44 @@
 
 
 def prepare_kernel(amp_ref, out_hbm, piece_ref, sems):
+    step = pl.program_id(0)
+    count = amp_ref.shape[0]
     width = piece_ref.shape[3] // 2
-    for g in range(NBLK):
+
+    def copies(part):
+        blocks = pl.ds(part * count, count)
+        return [
+            pltpu.make_async_copy(piece_ref.at[blocks], out_hbm.at[blocks, j], sems.at[part, j])
+            for j in range(RING)
+        ]
+
+    for g in range(count):
         for k in range(RING):
             for r in range(2):
-                piece_ref[g, k, :, r * width : (r + 1) * width] = amp_ref[g, r][
+                piece_ref[step * count + g, k, :, r * width : (r + 1) * width] = amp_ref[g, r][
                     :, k * width : (k + 1) * width
                 ]
-    copies = [
-        pltpu.make_async_copy(piece_ref, out_hbm.at[:, j], sems.at[j]) for j in range(RING)
-    ]
-    for copy in copies:
+    for copy in copies(step):
         copy.start()
-    for copy in copies:
-        copy.wait()
+
+    @pl.when(step == PARTS - 1)
+    def _():
+        for part in range(PARTS):
+            for copy in copies(part):
+                copy.wait()
 
 
 def prepare(amplitudes, width):
+    count = NBLK // PARTS
     return pl.pallas_call(
         prepare_kernel,
-        in_specs=[VMEM],
+        grid=(PARTS,),
+        in_specs=[pl.BlockSpec((count,) + amplitudes.shape[1:], lambda i: (i, 0, 0, 0))],
         out_specs=ANY,
         out_shape=jax.ShapeDtypeStruct((NBLK, RING, RING, 1, 2 * width), jnp.float32),
         scratch_shapes=[
             pltpu.VMEM((NBLK, RING, 1, 2 * width), jnp.float32),
-            pltpu.SemaphoreType.DMA((RING,)),
+            pltpu.SemaphoreType.DMA((PARTS, RING)),
         ],
         cost_estimate=cost(0, 5 * 4 * amplitudes.size),
         compiler_params=params(56),

time: 88.6 us -> 88.6 us (level)
  no operation moved by 1% of the time
where the time goes in v5:
time: 88.6 us; the launch traced here: 88.1 us
  starting transfers between devices  35.7 us (40%)
  waiting for transfers between devices  31.2 us (35%)
  Pallas kernels  14.3 us (16%)
  matrix products  5.76 us (7%)
  local copies, waits for them, and re-layouts  0.98 us (1%)
    all_to_all x1, starting transfers between devices, on_device(): got = lax.all_to_all(outgoing, YZX, split_axis=0, concat_axis=0, tiled=True)  16.3 us
    all_to_all x1, waiting for transfers between devices, on_device(): got = lax.all_to_all(outgoing, YZX, split_axis=0, concat_axis=0, tiled=True)  16.1 us
    pallas_call x1, Pallas kernels, split_tile(): pl.pallas_call(split_kernel, grid=(10,), in_specs=[SMEM, pl.BlockSpec((ro...  9.75 us
    all_to_all x1, waiting for transfers between devices, on_device(): lax.all_to_all(leaving, ('y', 'z'), split_axis=0, concat_axis=0, tiled=True)  9.65 us
    ppermute x6, starting transfers between devices, shift(): return lax.ppermute(value, axis, [(i, (i + by) % n) for i in range(n)])  6.97 us
    ppermute x6, waiting for transfers between devices, shift(): return lax.ppermute(value, axis, [(i, (i + by) % n) for i in range(n)])  4.44 us
    ppermute x1, starting transfers between devices, on_device(): other = lax.ppermute(theirs, 'rep', SWAP)  4.33 us
    all_to_all x1, starting transfers between devices, on_device(): lax.all_to_all(leaving, ('y', 'z'), split_axis=0, concat_axis=0, tiled=True)  4.27 us
  transfers between devices with their start and end apart: 10, of which 5 were waited for; matrix products, arithmetic and copies ran while one was open for 3% of the time, Pallas kernels for 11%

profile of v5, /device:TPU:1, one launch (start us, length us, event | category | flops | bytes accessed | tf_op | source)
XLA Modules:
  0.0 88.1 jit_solution(17299173960438277705)
XLA Ops:
  0.0 2.1 %prepare.1 = f32[8,4,4,1,1920]{4,3,2,1,0:T(1,128)} custom-call(f32[8,2,1,3840]{3,2,1,0:T(1,128)} %amp_ref.1), custom_call_target="tpu_custom_call" | custom-call | bytes 1228800 | tf_op jit(solution)/shard_map/prepare/pallas_call | solution.py:77
  2.1 16.3 %all-to-all-start = ((f32[128,1,1920]{2,1,0:T(1,128)}), f32[128,1,1920]{2,1,0:T(1,128)S(1)}, u32[]{:S(2)}, u32[]{:S(2)}) async-start(f32[128,1,1920]{2,1,0:T(1,128)} %bitcast.38), calls=%async_computation | async-start | bytes 1966080 | tf_op jit(solution)/shard_map/all_to_all | solution.py:221
  18.5 0.0 copy-start
  18.5 9.7 %split_tile.1 = (bf16[960,1024]{1,0:T(8,128)(2,1)}, bf16[960,1024]{1,0:T(8,128)(2,1)}, bf16[960,1024]{1,0:T(8,128)(2,1)}, bf16[960,1024]{1,0:T(8,128)(2,1)}) custom-call(s32[8]{0:T(128)} %count_ref.3, f32[960,1920]{1,0:T(8,128)} %bitcast.34), custom_call_target="tpu_custom_call" | custom-call | flops 7372800 | bytes 14745600 | tf_op jit(solution)/shard_map/split_tile/pallas_call | solution.py:111
  28.3 16.1 %all-to-all-done = f32[128,1,1920]{2,1,0:T(1,128)S(1)} async-done(((f32[128,1,1920]{2,1,0:T(1,128)}), f32[128,1,1920]{2,1,0:T(1,128)S(1)}, u32[]{:S(2)}, u32[]{:S(2)}) %all-to-all-start) | async-done | bytes 983072 | tf_op jit(solution)/shard_map/all_to_all | solution.py:221
  44.4 0.9 %arrange.1 = bf16[512,960]{1,0:T(8,128)(2,1)S(1)} custom-call(s32[8]{0:T(128)S(1)} %copy-done, f32[32,4,1,1920]{3,2,1,0:T(1,128)S(1)} %bitcast.30), custom_call_target="tpu_custom_call" | custom-call | bytes 1966080 | tf_op jit(solution)/shard_map/arrange/pallas_call | solution.py:143
  45.3 0.6 copy-done.3
  45.9 1.3 %fusion.8 = f32[512,1024]{1,0:T(8,128)S(1)} fusion(bf16[512,960]{1,0:T(8,128)(2,1)S(1)} %arrange.1, bf16[960,1024]{1,0:T(8,128)(2,1)S(1)} %copy-done.3), kind=kOutput, calls=%fused_computation.18 | convolution fusion | flops 1006632960 | bytes 5046272 | tf_op jit(solution)/shard_map/dot_general | solution.py:157
  47.2 0.3 copy-done.1
  47.4 0.7 fusion
  48.2 3.8 %collective-permute-start = (f32[256,1024]{1,0:T(8,128)S(1)}, f32[256,1024]{1,0:T(8,128)S(1)}, u32[]{:S(2)}, u32[]{:S(2)}) collective-permute-start(f32[256,1024]{1,0:T(8,128)S(1)} %fusion), channel_id=1, source_target_pairs={{0,1},{1,0},{2,3},{3,2},{4,5},{5,4},{6,7},{7,6},{8,9},{9,8},{10,11... | collective-permute-start | bytes 3145736 | tf_op jit(solution)/shard_map/ppermute | solution.py:225
  52.0 2.9 %fusion.7 = f32[512,1024]{1,0:T(8,128)S(1)} fusion(bf16[512,960]{1,0:T(8,128)(2,1)S(1)} %arrange.1, bf16[960,1024]{1,0:T(8,128)(2,1)} %get-tuple-element.19), kind=kOutput, calls=%fused_computation.17 | convolution fusion | flops 1006632960 | bytes 5046272 | tf_op jit(solution)/shard_map/dot_general | solution.py:157
  54.9 0.0 collective-permute-done
  54.9 0.8 fusion.2
  55.8 0.1 dynamic-slice_bitcast_fusion
  55.8 0.2 collective-permute-start.2
  56.0 2.5 %collective-permute-start.4 = (f32[32,1024]{1,0:T(8,128)S(1)}, f32[32,1024]{1,0:T(8,128)S(1)}, u32[]{:S(2)}, u32[]{:S(2)}) collective-permute-start(f32[32,1024]{1,0:T(8,128)S(1)} %get-tuple-element.26), channel_id=1, source_target_pairs={{0,6},{2,0},{4,2},{6,4},{1,7},{3,1},{5,3},{7,5},{8,14},{10,8},{12,... | collective-permute-start | bytes 393224 | tf_op jit(solution)/shard_map/ppermute | solution.py:28
  58.6 0.0 collective-permute-start.1
  58.6 1.4 %collective-permute-start.6 = (f32[32,1024]{1,0:T(8,128)S(1)}, f32[32,1024]{1,0:T(8,128)S(1)}, u32[]{:S(2)}, u32[]{:S(2)}) collective-permute-start(f32[32,1024]{1,0:T(8,128)S(1)} %get-tuple-element.23), channel_id=1, source_target_pairs={{0,2},{2,4},{4,6},{6,0},{1,3},{3,5},{5,7},{7,1},{8,10},{10,12},{12... | collective-permute-start | bytes 393224 | tf_op jit(solution)/shard_map/ppermute | solution.py:28
  60.0 2.1 %collective-permute-done.2 = f32[32,1024]{1,0:T(8,128)S(1)} collective-permute-done((f32[32,1024]{1,0:T(8,128)S(1)}, f32[32,1024]{1,0:T(8,128)S(1)}, u32[]{:S(2)}, u32[]{:S(2)}) %collective-permute-start.2) | collective-permute-done | bytes 131104 | tf_op jit(solution)/shard_map/ppermute | solution.py:28
  62.2 0.0 collective-permute-done.4
  62.2 0.1 collective-permute-start.3
  62.3 2.7 %collective-permute-start.5 = (f32[32,1024]{1,0:T(8,128)S(1)}, f32[32,1024]{1,0:T(8,128)S(1)}, u32[]{:S(2)}, u32[]{:S(2)}) collective-permute-start(f32[32,1024]{1,0:T(8,128)S(1)} %get-tuple-element.27), channel_id=1, source_target_pairs={{0,6},{2,0},{4,2},{6,4},{1,7},{3,1},{5,3},{7,5},{8,14},{10,8},{12,... | collective-permute-start | bytes 393224 | tf_op jit(solution)/shard_map/ppermute | solution.py:28
  65.0 0.0 collective-permute-done.1.left_a
  65.0 0.0 collective-permute-done.6.right_b
  65.0 2.3 %collective-permute-done.3.right_a = f32[32,1024]{1,0:T(8,128)S(1)} collective-permute-done((f32[32,1024]{1,0:T(8,128)S(1)}, f32[32,1024]{1,0:T(8,128)S(1)}, u32[]{:S(2)}, u32[]{:S(2)}) %collective-permute-start.3) | collective-permute-done | bytes 131104 | tf_op jit(solution)/shard_map/ppermute | solution.py:28
  67.3 0.8 gather_rows.1
  68.1 4.3 %all-to-all-start.1 = ((f32[32,2,1024]{2,1,0:T(2,128)}), f32[32,2,1024]{2,1,0:T(2,128)S(1)}, u32[]{:S(2)}, u32[]{:S(2)}) async-start(f32[32,2,1024]{2,1,0:T(2,128)} %gather_rows.1), calls=%async_computation.1 | async-start | bytes 524288 | tf_op jit(solution)/shard_map/all_to_all | solution.py:236
  72.4 9.7 %all-to-all-done.1 = f32[32,2,1024]{2,1,0:T(2,128)S(1)} async-done(((f32[32,2,1024]{2,1,0:T(2,128)}), f32[32,2,1024]{2,1,0:T(2,128)S(1)}, u32[]{:S(2)}, u32[]{:S(2)}) %all-to-all-start.1) | async-done | bytes 262176 | tf_op jit(solution)/shard_map/all_to_all | solution.py:236
  82.0 4.3 %collective-permute-start.7 = (f32[8,2,2,1024]{3,2,1,0:T(2,128)S(1)}, f32[8,2,2,1024]{3,2,1,0:T(2,128)S(1)}, u32[]{:S(2)}, u32[]{:S(2)}) collective-permute-start(f32[8,2,2,1024]{3,2,1,0:T(2,128)S(1)} %constant_dynamic-slice_fusion), channel_id=1, source_target_pairs={{0,1},{1,0},{2,3},{3,2},{4,5},{5,4},{6,7},{7,6},{8,9},{9,8},{10,11... | collective-permute-start | bytes 393224 | tf_op jit(solution)/shard_map/ppermute | solution.py:239
  86.4 1.0 %collective-permute-done.7.other_ref = f32[8,2,2,1024]{3,2,1,0:T(2,128)S(1)} collective-permute-done((f32[8,2,2,1024]{3,2,1,0:T(2,128)S(1)}, f32[8,2,2,1024]{3,2,1,0:T(2,128)S(1)}, u32[]{:S(2)}, u32[]{:S(2)}) %collective-permute-start.7) | collective-permute-done | bytes 131104 | tf_op jit(solution)/shard_map/ppermute | solution.py:239
  87.3 0.7 final_rows.1
  (9 shorter events, 0.1 us)
Async XLA Ops:
  2.1 42.2 %all-to-all-start = ((f32[128,1,1920]{2,1,0:T(1,128)}), f32[128,1,1920]{2,1,0:T(1,128)S(1)}, u32[]{:S(2)}, u32[]{:S(2)}) async-start(f32[128,1,1920]{2,1,0:T(1,128)} %bitcast.38), calls=%async_computation | async-start | bytes 1966080 | tf_op jit(solution)/shard_map/all_to_all | solution.py:221
  18.5 25.9 %copy-start = (s32[8]{0:T(128)S(1)}, s32[8]{0:T(128)}, u32[]{:S(2)}) copy-start(s32[8]{0:T(128)} %count_ref.3) | copy-start | bytes 100
  44.4 1.5 %copy-start.3 = (bf16[960,1024]{1,0:T(8,128)(2,1)S(1)}, bf16[960,1024]{1,0:T(8,128)(2,1)}, u32[]{:S(2)}) copy-start(bf16[960,1024]{1,0:T(8,128)(2,1)} %get-tuple-element.21) | copy-start | bytes 5898244
  45.9 1.5 %copy-start.1 = (bf16[960,1024]{1,0:T(8,128)(2,1)S(1)}, bf16[960,1024]{1,0:T(8,128)(2,1)}, u32[]{:S(2)}) copy-start(bf16[960,1024]{1,0:T(8,128)(2,1)} %get-tuple-element.22) | copy-start | bytes 5898244
  48.2 6.7 %collective-permute-start = (f32[256,1024]{1,0:T(8,128)S(1)}, f32[256,1024]{1,0:T(8,128)S(1)}, u32[]{:S(2)}, u32[]{:S(2)}) collective-permute-start(f32[256,1024]{1,0:T(8,128)S(1)} %fusion), channel_id=1, source_target_pairs={{0,1},{1,0},{2,3},{3,2},{4,5},{5,4},{6,7},{7,6},{8,9},{9,8},{10,11... | collective-permute-start | bytes 3145736 | tf_op jit(solution)/shard_map/ppermute | solution.py:225
  52.0 3.0 %copy-start.2 = (bf16[960,1024]{1,0:T(8,128)(2,1)S(1)}, bf16[960,1024]{1,0:T(8,128)(2,1)}, u32[]{:S(2)}) copy-start(bf16[960,1024]{1,0:T(8,128)(2,1)} %get-tuple-element.20) | copy-start | bytes 5898244
  55.8 6.3 %collective-permute-start.2 = (f32[32,1024]{1,0:T(8,128)S(1)}, f32[32,1024]{1,0:T(8,128)S(1)}, u32[]{:S(2)}, u32[]{:S(2)}) collective-permute-start(f32[32,1024]{1,0:T(8,128)S(1)} %get-tuple-element.24), channel_id=1, source_target_pairs={{0,2},{2,4},{4,6},{6,0},{1,3},{3,5},{5,7},{7,1},{8,10},{10,12},{12... | collective-permute-start | bytes 393224 | tf_op jit(solution)/shard_map/ppermute | solution.py:28
  56.0 6.1 %collective-permute-start.4 = (f32[32,1024]{1,0:T(8,128)S(1)}, f32[32,1024]{1,0:T(8,128)S(1)}, u32[]{:S(2)}, u32[]{:S(2)}) collective-permute-start(f32[32,1024]{1,0:T(8,128)S(1)} %get-tuple-element.26), channel_id=1, source_target_pairs={{0,6},{2,0},{4,2},{6,4},{1,7},{3,1},{5,3},{7,5},{8,14},{10,8},{12,... | collective-permute-start | bytes 393224 | tf_op jit(solution)/shard_map/ppermute | solution.py:28
  58.6 6.4 %collective-permute-start.1 = (f32[32,1024]{1,0:T(8,128)S(1)}, f32[32,1024]{1,0:T(8,128)S(1)}, u32[]{:S(2)}, u32[]{:S(2)}) collective-permute-start(f32[32,1024]{1,0:T(8,128)S(1)} %get-tuple-element.25), channel_id=1, source_target_pairs={{0,6},{2,0},{4,2},{6,4},{1,7},{3,1},{5,3},{7,5},{8,14},{10,8},{12,... | collective-permute-start | bytes 393224 | tf_op jit(solution)/shard_map/ppermute | solution.py:28
  58.6 6.4 %collective-permute-start.6 = (f32[32,1024]{1,0:T(8,128)S(1)}, f32[32,1024]{1,0:T(8,128)S(1)}, u32[]{:S(2)}, u32[]{:S(2)}) collective-permute-start(f32[32,1024]{1,0:T(8,128)S(1)} %get-tuple-element.23), channel_id=1, source_target_pairs={{0,2},{2,4},{4,6},{6,0},{1,3},{3,5},{5,7},{7,1},{8,10},{10,12},{12... | collective-permute-start | bytes 393224 | tf_op jit(solution)/shard_map/ppermute | solution.py:28
  62.2 5.1 %collective-permute-start.3 = (f32[32,1024]{1,0:T(8,128)S(1)}, f32[32,1024]{1,0:T(8,128)S(1)}, u32[]{:S(2)}, u32[]{:S(2)}) collective-permute-start(f32[32,1024]{1,0:T(8,128)S(1)} %get-tuple-element.28), channel_id=1, source_target_pairs={{0,2},{2,4},{4,6},{6,0},{1,3},{3,5},{5,7},{7,1},{8,10},{10,12},{12... | collective-permute-start | bytes 393224 | tf_op jit(solution)/shard_map/ppermute | solution.py:28
  62.3 5.0 %collective-permute-start.5 = (f32[32,1024]{1,0:T(8,128)S(1)}, f32[32,1024]{1,0:T(8,128)S(1)}, u32[]{:S(2)}, u32[]{:S(2)}) collective-permute-start(f32[32,1024]{1,0:T(8,128)S(1)} %get-tuple-element.27), channel_id=1, source_target_pairs={{0,6},{2,0},{4,2},{6,4},{1,7},{3,1},{5,3},{7,5},{8,14},{10,8},{12,... | collective-permute-start | bytes 393224 | tf_op jit(solution)/shard_map/ppermute | solution.py:28
  68.1 13.9 %all-to-all-start.1 = ((f32[32,2,1024]{2,1,0:T(2,128)}), f32[32,2,1024]{2,1,0:T(2,128)S(1)}, u32[]{:S(2)}, u32[]{:S(2)}) async-start(f32[32,2,1024]{2,1,0:T(2,128)} %gather_rows.1), calls=%async_computation.1 | async-start | bytes 524288 | tf_op jit(solution)/shard_map/all_to_all | solution.py:236
  82.0 5.3 %collective-permute-start.7 = (f32[8,2,2,1024]{3,2,1,0:T(2,128)S(1)}, f32[8,2,2,1024]{3,2,1,0:T(2,128)S(1)}, u32[]{:S(2)}, u32[]{:S(2)}) collective-permute-start(f32[8,2,2,1024]{3,2,1,0:T(2,128)S(1)} %constant_dynamic-slice_fusion), channel_id=1, source_target_pairs={{0,1},{1,0},{2,3},{3,2},{4,5},{5,4},{6,7},{7,6},{8,9},{9,8},{10,11... | collective-permute-start | bytes 393224 | tf_op jit(solution)/shard_map/ppermute | solution.py:239
